TPU v7x, 256 devices: a whole 4x4x8 slice. The times are simulated.
256 devices in a mesh: tm: 128 (over y, x, z), space: 2 (over core).
Axes of the slice: x: 4, y: 4, z: 8, core: 2. Of those that a mesh axis runs over, the one named last changes fastest.
Arguments:
- forcing: float32 [128, 512, 8, 256], P('tm', None, None, 'space'), may hold values from -6 to 6
- initial: float32 [512, 64, 256], P('tm', None, 'space'), may hold values from -6 to 6
- diffusion: float32 [512, 64, 256], P('tm', None, 'space'), may hold values from 0.25 to 4
- drift: float32 [512, 64, 256], P('tm', None, 'space'), may hold values from 0.2 to 1.5
Outputs:
- states: float32 [128, 512, 8, 256], P('tm', None, None, 'space')
All inputs are finite; a program needn't handle non-finite values.
Results may differ from a plain program's by a relative error of at most 0.00002.
Values sent between devices are 32-bit elements; how exact they have to be, the bound alone decides.
A program may use at most 64 MiB of HBM per device.

v0:
```python
import jax
import jax.numpy as jnp
from jax import lax
from jax.sharding import PartitionSpec as P

NT = 16


def padded(shard, sides, width):
    for axis, dim in sides:
        size, length = (lax.axis_size(axis), shard.shape[dim])
        up = [(i, (i + 1) % size) for i in range(size - 1)]
        down = [(j, i) for i, j in up]
        last = lax.slice_in_dim(shard, length - width, length, axis=dim)
        leading = lax.slice_in_dim(shard, 0, width, axis=dim)
        before = lax.ppermute(last, axis, up)
        after = lax.ppermute(leading, axis, down)
        shard = jnp.concatenate([before, shard, after], axis=dim)
    return shard


def relax_cells(field, source, diffus, drift_rate):
    widened = jnp.pad(field, ((0, 0), (1, 1), (0, 0)))
    beside = field[2:, :, 1:-1] + field[:-2, :, 1:-1]
    beside = beside + field[1:-1, :, 2:] + field[1:-1, :, :-2]
    beside = beside + widened[1:-1, 2:, 1:-1] + widened[1:-1, :-2, 1:-1]
    upstream = field[:-2, :, 1:-1]
    return (source + diffus * beside + drift_rate * upstream) / (1.0 + 6.0 * diffus + drift_rate)


def trim_rim(values, margin_cut):
    zlen = values.shape[-3]
    ylen = values.shape[-1]
    return values[..., margin_cut : zlen - margin_cut, :, margin_cut : ylen - margin_cut]


def sweep_block(widened, coef_wide, depth):
    grown = widened[0]
    for inner in range(depth):
        margin_cut = inner + 1
        grown = relax_cells(
            grown,
            trim_rim(widened[1], margin_cut),
            trim_rim(coef_wide[0], margin_cut),
            trim_rim(coef_wide[1], margin_cut),
        )
    return grown


def per_device(forcing, initial, diffusion, drift):
    xparts = lax.axis_size("tm") // NT
    slabs = lax.all_to_all(forcing, "tm", split_axis=1, concat_axis=0, tiled=True)
    zcells = slabs.shape[1]
    xpart = slabs.shape[2]
    ycells = slabs.shape[3]
    slabs = slabs.reshape(NT, xparts, zcells, xpart, ycells).transpose(0, 2, 1, 3, 4)
    slabs = slabs.reshape(NT, zcells, xparts * xpart, ycells)
    coeffs = jnp.stack((diffusion, drift))
    coef_wide = padded(coeffs, (("tm", 1), ("space", 3)), 4)

    def advance(current, forcing_now):
        source = current + forcing_now
        field = current
        widened = padded(jnp.stack((field, source)), (("tm", 1), ("space", 3)), 4)
        field = sweep_block(widened, coef_wide, 4)
        return (field, field)

    final, result = lax.scan(advance, initial, slabs)
    result = result.reshape(NT, zcells, xparts, xpart, ycells).transpose(0, 2, 1, 3, 4)
    result = result.reshape(NT * xparts, zcells, xpart, ycells)
    return lax.all_to_all(result, "tm", split_axis=0, concat_axis=1, tiled=True)


def solution(mesh):
    in_specs = (
        P("tm", None, None, "space"),
        P("tm", None, "space"),
        P("tm", None, "space"),
        P("tm", None, "space"),
    )
    out_specs = P("tm", None, None, "space")
    return jax.shard_map(
        per_device, mesh=mesh, in_specs=in_specs, out_specs=out_specs, check_vma=False
    )
```

profile of v0, /device:TPU:31, one launch (start us, length us, event | category | flops | bytes accessed | tf_op | source)
XLA Modules:
  0.0 660.2 jit_solution(16492417778323185253)
XLA Ops:
  0.0 15.3 %all-to-all-start = ((f32[1,512,8,128]{3,2,0,1:T(8,128)}), f32[1,512,8,128]{3,2,0,1:T(8,128)S(1)}, u32[]{:S(2)}, u32[]{:S(2)}) async-start(f32[1,512,8,128]{3,2,0,1:T(8,128)} %bitcast.56), calls=%async_computation | async-start | bytes 4194304 | tf_op jit(solution)/shard_map/all_to_all | solution.py:52
  15.7 3.1 collective-permute-start.4
  18.8 4.3 collective-permute-start.5
  23.1 50.5 %collective-permute-done.4 = f32[2,4,64,128]{2,3,1,0:T(8,128)S(1)} collective-permute-done((f32[2,4,64,128]{2,3,1,0:T(8,128)S(1)}, f32[2,4,64,128]{2,3,1,0:T(8,128)S(1)}, u32[]{:S(2)}, u32[]{:S(2)}) %collective-permute-start.4) | collective-permute-done | bytes 262176 | tf_op jit(solution)/shard_map/ppermute | solution.py:16
  76.3 4.7 collective-permute-start.7
  85.7 480.9 %while.14 = (s32[]{:T(128)}, f32[4,64,128]{1,2,0:T(8,128)S(1)}, f32[16,4,64,128]{3,2,1,0:T(8,128)}, f32[16,4,64,128]{3,2,1,0:T(8,128)}, f32[2,12,64,136]{2,3,1,0:T(8,128)}, /*index=5*/s32[]{:T(128)}) while((s32[]{:T(128)}, f32[4,64,128]{1,2,0:T(8,128)S(1)}, f32[16,4,64,128]{3,2,1,0:T(8,128)}, f32[16,4,64,128]{3,2,1,0:T(8,128)}, ...), condition=%wide.region_1.2_spmd, body=%wide.region_0.1_spmd.sunk | while | flops 4248066 | bytes 30435600 | solution.py:68
  86.8 3.2 collective-permute-start
  92.3 9.8 %collective-permute-done = f32[2,4,64,128]{2,3,1,0:T(8,128)S(1)} collective-permute-done((f32[2,4,64,128]{2,3,1,0:T(8,128)S(1)}, f32[2,4,64,128]{2,3,1,0:T(8,128)S(1)}, u32[]{:S(2)}, u32[]{:S(2)}) %collective-permute-start) | collective-permute-done | bytes 262176 | tf_op jit(solution)/shard_map/while/body/eval_jaxpr/ppermute | solution.py:17
  102.0 4.9 collective-permute-done.1
  106.9 3.4 collective-permute-start.2
  120.0 3.4 collective-permute-start.1
  123.4 10.0 %collective-permute-done = f32[2,4,64,128]{2,3,1,0:T(8,128)S(1)} collective-permute-done((f32[2,4,64,128]{2,3,1,0:T(8,128)S(1)}, f32[2,4,64,128]{2,3,1,0:T(8,128)S(1)}, u32[]{:S(2)}, u32[]{:S(2)}) %collective-permute-start) | collective-permute-done | bytes 262176 | tf_op jit(solution)/shard_map/while/body/eval_jaxpr/ppermute | solution.py:17
  133.4 4.0 collective-permute-done.1
  137.5 2.9 collective-permute-start.2
  150.0 3.4 collective-permute-start.1
  153.4 10.0 %collective-permute-done = f32[2,4,64,128]{2,3,1,0:T(8,128)S(1)} collective-permute-done((f32[2,4,64,128]{2,3,1,0:T(8,128)S(1)}, f32[2,4,64,128]{2,3,1,0:T(8,128)S(1)}, u32[]{:S(2)}, u32[]{:S(2)}) %collective-permute-start) | collective-permute-done | bytes 262176 | tf_op jit(solution)/shard_map/while/body/eval_jaxpr/ppermute | solution.py:17
  163.4 4.0 collective-permute-done.1
  167.4 2.9 collective-permute-start.2
  180.0 3.4 collective-permute-start.1
  183.4 10.0 %collective-permute-done = f32[2,4,64,128]{2,3,1,0:T(8,128)S(1)} collective-permute-done((f32[2,4,64,128]{2,3,1,0:T(8,128)S(1)}, f32[2,4,64,128]{2,3,1,0:T(8,128)S(1)}, u32[]{:S(2)}, u32[]{:S(2)}) %collective-permute-start) | collective-permute-done | bytes 262176 | tf_op jit(solution)/shard_map/while/body/eval_jaxpr/ppermute | solution.py:17
  193.4 4.0 collective-permute-done.1
  197.4 2.9 collective-permute-start.2
  210.0 3.4 collective-permute-start.1
  213.4 10.0 %collective-permute-done = f32[2,4,64,128]{2,3,1,0:T(8,128)S(1)} collective-permute-done((f32[2,4,64,128]{2,3,1,0:T(8,128)S(1)}, f32[2,4,64,128]{2,3,1,0:T(8,128)S(1)}, u32[]{:S(2)}, u32[]{:S(2)}) %collective-permute-start) | collective-permute-done | bytes 262176 | tf_op jit(solution)/shard_map/while/body/eval_jaxpr/ppermute | solution.py:17
  223.3 4.0 collective-permute-done.1
  227.4 2.9 collective-permute-start.2
  240.0 3.4 collective-permute-start.1
  243.4 10.0 %collective-permute-done = f32[2,4,64,128]{2,3,1,0:T(8,128)S(1)} collective-permute-done((f32[2,4,64,128]{2,3,1,0:T(8,128)S(1)}, f32[2,4,64,128]{2,3,1,0:T(8,128)S(1)}, u32[]{:S(2)}, u32[]{:S(2)}) %collective-permute-start) | collective-permute-done | bytes 262176 | tf_op jit(solution)/shard_map/while/body/eval_jaxpr/ppermute | solution.py:17
  253.3 4.0 collective-permute-done.1
  257.4 2.9 collective-permute-start.2
  270.0 3.4 collective-permute-start.1
  273.3 10.0 %collective-permute-done = f32[2,4,64,128]{2,3,1,0:T(8,128)S(1)} collective-permute-done((f32[2,4,64,128]{2,3,1,0:T(8,128)S(1)}, f32[2,4,64,128]{2,3,1,0:T(8,128)S(1)}, u32[]{:S(2)}, u32[]{:S(2)}) %collective-permute-start) | collective-permute-done | bytes 262176 | tf_op jit(solution)/shard_map/while/body/eval_jaxpr/ppermute | solution.py:17
  283.3 4.0 collective-permute-done.1
  287.4 2.9 collective-permute-start.2
  300.0 3.4 collective-permute-start.1
  303.3 10.0 %collective-permute-done = f32[2,4,64,128]{2,3,1,0:T(8,128)S(1)} collective-permute-done((f32[2,4,64,128]{2,3,1,0:T(8,128)S(1)}, f32[2,4,64,128]{2,3,1,0:T(8,128)S(1)}, u32[]{:S(2)}, u32[]{:S(2)}) %collective-permute-start) | collective-permute-done | bytes 262176 | tf_op jit(solution)/shard_map/while/body/eval_jaxpr/ppermute | solution.py:17
  313.3 4.0 collective-permute-done.1
  317.4 2.9 collective-permute-start.2
  329.9 3.4 collective-permute-start.1
  333.3 10.0 %collective-permute-done = f32[2,4,64,128]{2,3,1,0:T(8,128)S(1)} collective-permute-done((f32[2,4,64,128]{2,3,1,0:T(8,128)S(1)}, f32[2,4,64,128]{2,3,1,0:T(8,128)S(1)}, u32[]{:S(2)}, u32[]{:S(2)}) %collective-permute-start) | collective-permute-done | bytes 262176 | tf_op jit(solution)/shard_map/while/body/eval_jaxpr/ppermute | solution.py:17
  343.3 4.0 collective-permute-done.1
  347.4 2.9 collective-permute-start.2
  359.9 3.4 collective-permute-start.1
  363.3 10.0 %collective-permute-done = f32[2,4,64,128]{2,3,1,0:T(8,128)S(1)} collective-permute-done((f32[2,4,64,128]{2,3,1,0:T(8,128)S(1)}, f32[2,4,64,128]{2,3,1,0:T(8,128)S(1)}, u32[]{:S(2)}, u32[]{:S(2)}) %collective-permute-start) | collective-permute-done | bytes 262176 | tf_op jit(solution)/shard_map/while/body/eval_jaxpr/ppermute | solution.py:17
  373.3 4.0 collective-permute-done.1
  389.9 3.4 collective-permute-start.1
  393.3 10.0 %collective-permute-done = f32[2,4,64,128]{2,3,1,0:T(8,128)S(1)} collective-permute-done((f32[2,4,64,128]{2,3,1,0:T(8,128)S(1)}, f32[2,4,64,128]{2,3,1,0:T(8,128)S(1)}, u32[]{:S(2)}, u32[]{:S(2)}) %collective-permute-start) | collective-permute-done | bytes 262176 | tf_op jit(solution)/shard_map/while/body/eval_jaxpr/ppermute | solution.py:17
  403.3 4.0 collective-permute-done.1
  419.9 3.4 collective-permute-start.1
  423.3 10.0 %collective-permute-done = f32[2,4,64,128]{2,3,1,0:T(8,128)S(1)} collective-permute-done((f32[2,4,64,128]{2,3,1,0:T(8,128)S(1)}, f32[2,4,64,128]{2,3,1,0:T(8,128)S(1)}, u32[]{:S(2)}, u32[]{:S(2)}) %collective-permute-start) | collective-permute-done | bytes 262176 | tf_op jit(solution)/shard_map/while/body/eval_jaxpr/ppermute | solution.py:17
  433.2 4.0 collective-permute-done.1
  449.9 3.4 collective-permute-start.1
  453.3 10.0 %collective-permute-done = f32[2,4,64,128]{2,3,1,0:T(8,128)S(1)} collective-permute-done((f32[2,4,64,128]{2,3,1,0:T(8,128)S(1)}, f32[2,4,64,128]{2,3,1,0:T(8,128)S(1)}, u32[]{:S(2)}, u32[]{:S(2)}) %collective-permute-start) | collective-permute-done | bytes 262176 | tf_op jit(solution)/shard_map/while/body/eval_jaxpr/ppermute | solution.py:17
  463.2 4.0 collective-permute-done.1
  479.9 3.4 collective-permute-start.1
  483.2 10.0 %collective-permute-done = f32[2,4,64,128]{2,3,1,0:T(8,128)S(1)} collective-permute-done((f32[2,4,64,128]{2,3,1,0:T(8,128)S(1)}, f32[2,4,64,128]{2,3,1,0:T(8,128)S(1)}, u32[]{:S(2)}, u32[]{:S(2)}) %collective-permute-start) | collective-permute-done | bytes 262176 | tf_op jit(solution)/shard_map/while/body/eval_jaxpr/ppermute | solution.py:17
  493.2 4.0 collective-permute-done.1
  509.9 3.4 collective-permute-start.1
  513.2 10.0 %collective-permute-done = f32[2,4,64,128]{2,3,1,0:T(8,128)S(1)} collective-permute-done((f32[2,4,64,128]{2,3,1,0:T(8,128)S(1)}, f32[2,4,64,128]{2,3,1,0:T(8,128)S(1)}, u32[]{:S(2)}, u32[]{:S(2)}) %collective-permute-start) | collective-permute-done | bytes 262176 | tf_op jit(solution)/shard_map/while/body/eval_jaxpr/ppermute | solution.py:17
  523.2 4.0 collective-permute-done.1
  539.8 3.4 collective-permute-start.1
  543.2 10.0 %collective-permute-done = f32[2,4,64,128]{2,3,1,0:T(8,128)S(1)} collective-permute-done((f32[2,4,64,128]{2,3,1,0:T(8,128)S(1)}, f32[2,4,64,128]{2,3,1,0:T(8,128)S(1)}, u32[]{:S(2)}, u32[]{:S(2)}) %collective-permute-start) | collective-permute-done | bytes 262176 | tf_op jit(solution)/shard_map/while/body/eval_jaxpr/ppermute | solution.py:17
  553.2 4.0 collective-permute-done.1
  568.5 90.4 %all_to_all.21 = f32[128,4,8,128]{3,2,1,0:T(8,128)S(1)} all-to-all(f32[128,4,8,128]{3,2,1,0:T(8,128)S(1)} %bitcast.47), channel_id=1, replica_groups=mesh['tm'=128,'space'=2] {'tm'}, dimensions={0} | all-to-all | bytes 4194304 | tf_op jit(solution)/shard_map/all_to_all | solution.py:71
  (350 shorter events, 185.1 us)
Async XLA Ops:
  0.0 84.1 %all-to-all-start = ((f32[1,512,8,128]{3,2,0,1:T(8,128)}), f32[1,512,8,128]{3,2,0,1:T(8,128)S(1)}, u32[]{:S(2)}, u32[]{:S(2)}) async-start(f32[1,512,8,128]{3,2,0,1:T(8,128)} %bitcast.56), calls=%async_computation | async-start | bytes 4194304 | tf_op jit(solution)/shard_map/all_to_all | solution.py:52
  15.7 57.9 %collective-permute-start.4 = (f32[2,4,64,128]{2,3,1,0:T(8,128)S(1)}, f32[2,4,64,128]{2,3,1,0:T(8,128)S(1)}, u32[]{:S(2)}, u32[]{:S(2)}) collective-permute-start(f32[2,4,64,128]{2,3,1,0:T(8,128)S(1)} %pad_maximum_fusion.7), channel_id=1, source_target_pairs={{0,2},{2,4},{4,6},{6,8},{8,10},{10,12},{12,14},{14,16},{16,18},{18... | collective-permute-start | bytes 786440 | tf_op jit(solution)/shard_map/ppermute | solution.py:16
  18.8 54.8 %collective-permute-start.5 = (f32[2,4,64,128]{2,3,1,0:T(8,128)S(1)}, f32[2,4,64,128]{2,3,1,0:T(8,128)S(1)}, u32[]{:S(2)}, u32[]{:S(2)}) collective-permute-start(f32[2,4,64,128]{2,3,1,0:T(8,128)S(1)} %pad_maximum_fusion.7), channel_id=1, source_target_pairs={{2,0},{4,2},{6,4},{8,6},{10,8},{12,10},{14,12},{16,14},{18,16},{20... | collective-permute-start | bytes 786440 | tf_op jit(solution)/shard_map/ppermute | solution.py:17
  75.0 6.2 collective-permute-start.6
  76.3 5.3 collective-permute-start.7
  86.8 15.2 %collective-permute-start = (f32[2,4,64,128]{2,3,1,0:T(8,128)S(1)}, f32[2,4,64,128]{2,3,1,0:T(8,128)S(1)}, u32[]{:S(2)}, u32[]{:S(2)}) collective-permute-start(f32[2,4,64,128]{2,3,1,0:T(8,128)S(1)} %pad_maximum_fusion.15), channel_id=1, source_target_pairs={{2,0},{4,2},{6,4},{8,6},{10,8},{12,10},{14,12},{16,14},{18,16},{20... | collective-permute-start | bytes 786440 | tf_op jit(solution)/shard_map/while/body/eval_jaxpr/ppermute | solution.py:17
  90.1 16.8 %collective-permute-start.1 = (f32[2,4,64,128]{2,3,1,0:T(8,128)S(1)}, f32[2,4,64,128]{2,3,1,0:T(8,128)S(1)}, u32[]{:S(2)}, u32[]{:S(2)}) collective-permute-start(f32[2,4,64,128]{2,3,1,0:T(8,128)S(1)} %pad_maximum_fusion.15), channel_id=1, source_target_pairs={{0,2},{2,4},{4,6},{6,8},{8,10},{10,12},{12,14},{14,16},{16,18},{18... | collective-permute-start | bytes 786440 | tf_op jit(solution)/shard_map/while/body/eval_jaxpr/ppermute | solution.py:16
  106.9 4.8 collective-permute-start.2
  110.3 3.1 collective-permute-start.3
  118.0 15.4 %collective-permute-start = (f32[2,4,64,128]{2,3,1,0:T(8,128)S(1)}, f32[2,4,64,128]{2,3,1,0:T(8,128)S(1)}, u32[]{:S(2)}, u32[]{:S(2)}) collective-permute-start(f32[2,4,64,128]{2,3,1,0:T(8,128)S(1)} %pad_maximum_fusion.15), channel_id=1, source_target_pairs={{2,0},{4,2},{6,4},{8,6},{10,8},{12,10},{14,12},{16,14},{18,16},{20... | collective-permute-start | bytes 786440 | tf_op jit(solution)/shard_map/while/body/eval_jaxpr/ppermute | solution.py:17
  120.0 17.4 %collective-permute-start.1 = (f32[2,4,64,128]{2,3,1,0:T(8,128)S(1)}, f32[2,4,64,128]{2,3,1,0:T(8,128)S(1)}, u32[]{:S(2)}, u32[]{:S(2)}) collective-permute-start(f32[2,4,64,128]{2,3,1,0:T(8,128)S(1)} %pad_maximum_fusion.15), channel_id=1, source_target_pairs={{0,2},{2,4},{4,6},{6,8},{8,10},{10,12},{12,14},{14,16},{16,18},{18... | collective-permute-start | bytes 786440 | tf_op jit(solution)/shard_map/while/body/eval_jaxpr/ppermute | solution.py:16
  137.5 4.3 collective-permute-start.2
  140.3 3.1 collective-permute-start.3
  148.0 15.4 %collective-permute-start = (f32[2,4,64,128]{2,3,1,0:T(8,128)S(1)}, f32[2,4,64,128]{2,3,1,0:T(8,128)S(1)}, u32[]{:S(2)}, u32[]{:S(2)}) collective-permute-start(f32[2,4,64,128]{2,3,1,0:T(8,128)S(1)} %pad_maximum_fusion.15), channel_id=1, source_target_pairs={{2,0},{4,2},{6,4},{8,6},{10,8},{12,10},{14,12},{16,14},{18,16},{20... | collective-permute-start | bytes 786440 | tf_op jit(solution)/shard_map/while/body/eval_jaxpr/ppermute | solution.py:17
  150.0 17.4 %collective-permute-start.1 = (f32[2,4,64,128]{2,3,1,0:T(8,128)S(1)}, f32[2,4,64,128]{2,3,1,0:T(8,128)S(1)}, u32[]{:S(2)}, u32[]{:S(2)}) collective-permute-start(f32[2,4,64,128]{2,3,1,0:T(8,128)S(1)} %pad_maximum_fusion.15), channel_id=1, source_target_pairs={{0,2},{2,4},{4,6},{6,8},{8,10},{10,12},{12,14},{14,16},{16,18},{18... | collective-permute-start | bytes 786440 | tf_op jit(solution)/shard_map/while/body/eval_jaxpr/ppermute | solution.py:16
  167.4 4.3 collective-permute-start.2
  178.0 15.4 %collective-permute-start = (f32[2,4,64,128]{2,3,1,0:T(8,128)S(1)}, f32[2,4,64,128]{2,3,1,0:T(8,128)S(1)}, u32[]{:S(2)}, u32[]{:S(2)}) collective-permute-start(f32[2,4,64,128]{2,3,1,0:T(8,128)S(1)} %pad_maximum_fusion.15), channel_id=1, source_target_pairs={{2,0},{4,2},{6,4},{8,6},{10,8},{12,10},{14,12},{16,14},{18,16},{20... | collective-permute-start | bytes 786440 | tf_op jit(solution)/shard_map/while/body/eval_jaxpr/ppermute | solution.py:17
  180.0 17.4 %collective-permute-start.1 = (f32[2,4,64,128]{2,3,1,0:T(8,128)S(1)}, f32[2,4,64,128]{2,3,1,0:T(8,128)S(1)}, u32[]{:S(2)}, u32[]{:S(2)}) collective-permute-start(f32[2,4,64,128]{2,3,1,0:T(8,128)S(1)} %pad_maximum_fusion.15), channel_id=1, source_target_pairs={{0,2},{2,4},{4,6},{6,8},{8,10},{10,12},{12,14},{14,16},{16,18},{18... | collective-permute-start | bytes 786440 | tf_op jit(solution)/shard_map/while/body/eval_jaxpr/ppermute | solution.py:16
  197.4 4.3 collective-permute-start.2
  200.3 3.1 collective-permute-start.3
  207.9 15.4 %collective-permute-start = (f32[2,4,64,128]{2,3,1,0:T(8,128)S(1)}, f32[2,4,64,128]{2,3,1,0:T(8,128)S(1)}, u32[]{:S(2)}, u32[]{:S(2)}) collective-permute-start(f32[2,4,64,128]{2,3,1,0:T(8,128)S(1)} %pad_maximum_fusion.15), channel_id=1, source_target_pairs={{2,0},{4,2},{6,4},{8,6},{10,8},{12,10},{14,12},{16,14},{18,16},{20... | collective-permute-start | bytes 786440 | tf_op jit(solution)/shard_map/while/body/eval_jaxpr/ppermute | solution.py:17
  210.0 17.4 %collective-permute-start.1 = (f32[2,4,64,128]{2,3,1,0:T(8,128)S(1)}, f32[2,4,64,128]{2,3,1,0:T(8,128)S(1)}, u32[]{:S(2)}, u32[]{:S(2)}) collective-permute-start(f32[2,4,64,128]{2,3,1,0:T(8,128)S(1)} %pad_maximum_fusion.15), channel_id=1, source_target_pairs={{0,2},{2,4},{4,6},{6,8},{8,10},{10,12},{12,14},{14,16},{16,18},{18... | collective-permute-start | bytes 786440 | tf_op jit(solution)/shard_map/while/body/eval_jaxpr/ppermute | solution.py:16
  227.4 4.3 collective-permute-start.2
  237.9 15.4 %collective-permute-start = (f32[2,4,64,128]{2,3,1,0:T(8,128)S(1)}, f32[2,4,64,128]{2,3,1,0:T(8,128)S(1)}, u32[]{:S(2)}, u32[]{:S(2)}) collective-permute-start(f32[2,4,64,128]{2,3,1,0:T(8,128)S(1)} %pad_maximum_fusion.15), channel_id=1, source_target_pairs={{2,0},{4,2},{6,4},{8,6},{10,8},{12,10},{14,12},{16,14},{18,16},{20... | collective-permute-start | bytes 786440 | tf_op jit(solution)/shard_map/while/body/eval_jaxpr/ppermute | solution.py:17
  240.0 17.4 %collective-permute-start.1 = (f32[2,4,64,128]{2,3,1,0:T(8,128)S(1)}, f32[2,4,64,128]{2,3,1,0:T(8,128)S(1)}, u32[]{:S(2)}, u32[]{:S(2)}) collective-permute-start(f32[2,4,64,128]{2,3,1,0:T(8,128)S(1)} %pad_maximum_fusion.15), channel_id=1, source_target_pairs={{0,2},{2,4},{4,6},{6,8},{8,10},{10,12},{12,14},{14,16},{16,18},{18... | collective-permute-start | bytes 786440 | tf_op jit(solution)/shard_map/while/body/eval_jaxpr/ppermute | solution.py:16
  257.4 4.3 collective-permute-start.2
  260.3 3.1 collective-permute-start.3
  267.9 15.4 %collective-permute-start = (f32[2,4,64,128]{2,3,1,0:T(8,128)S(1)}, f32[2,4,64,128]{2,3,1,0:T(8,128)S(1)}, u32[]{:S(2)}, u32[]{:S(2)}) collective-permute-start(f32[2,4,64,128]{2,3,1,0:T(8,128)S(1)} %pad_maximum_fusion.15), channel_id=1, source_target_pairs={{2,0},{4,2},{6,4},{8,6},{10,8},{12,10},{14,12},{16,14},{18,16},{20... | collective-permute-start | bytes 786440 | tf_op jit(solution)/shard_map/while/body/eval_jaxpr/ppermute | solution.py:17
  270.0 17.4 %collective-permute-start.1 = (f32[2,4,64,128]{2,3,1,0:T(8,128)S(1)}, f32[2,4,64,128]{2,3,1,0:T(8,128)S(1)}, u32[]{:S(2)}, u32[]{:S(2)}) collective-permute-start(f32[2,4,64,128]{2,3,1,0:T(8,128)S(1)} %pad_maximum_fusion.15), channel_id=1, source_target_pairs={{0,2},{2,4},{4,6},{6,8},{8,10},{10,12},{12,14},{14,16},{16,18},{18... | collective-permute-start | bytes 786440 | tf_op jit(solution)/shard_map/while/body/eval_jaxpr/ppermute | solution.py:16
  287.4 4.3 collective-permute-start.2
  297.9 15.4 %collective-permute-start = (f32[2,4,64,128]{2,3,1,0:T(8,128)S(1)}, f32[2,4,64,128]{2,3,1,0:T(8,128)S(1)}, u32[]{:S(2)}, u32[]{:S(2)}) collective-permute-start(f32[2,4,64,128]{2,3,1,0:T(8,128)S(1)} %pad_maximum_fusion.15), channel_id=1, source_target_pairs={{2,0},{4,2},{6,4},{8,6},{10,8},{12,10},{14,12},{16,14},{18,16},{20... | collective-permute-start | bytes 786440 | tf_op jit(solution)/shard_map/while/body/eval_jaxpr/ppermute | solution.py:17
  300.0 17.4 %collective-permute-start.1 = (f32[2,4,64,128]{2,3,1,0:T(8,128)S(1)}, f32[2,4,64,128]{2,3,1,0:T(8,128)S(1)}, u32[]{:S(2)}, u32[]{:S(2)}) collective-permute-start(f32[2,4,64,128]{2,3,1,0:T(8,128)S(1)} %pad_maximum_fusion.15), channel_id=1, source_target_pairs={{0,2},{2,4},{4,6},{6,8},{8,10},{10,12},{12,14},{14,16},{16,18},{18... | collective-permute-start | bytes 786440 | tf_op jit(solution)/shard_map/while/body/eval_jaxpr/ppermute | solution.py:16
  317.4 4.3 collective-permute-start.2
  320.2 3.1 collective-permute-start.3
  327.9 15.4 %collective-permute-start = (f32[2,4,64,128]{2,3,1,0:T(8,128)S(1)}, f32[2,4,64,128]{2,3,1,0:T(8,128)S(1)}, u32[]{:S(2)}, u32[]{:S(2)}) collective-permute-start(f32[2,4,64,128]{2,3,1,0:T(8,128)S(1)} %pad_maximum_fusion.15), channel_id=1, source_target_pairs={{2,0},{4,2},{6,4},{8,6},{10,8},{12,10},{14,12},{16,14},{18,16},{20... | collective-permute-start | bytes 786440 | tf_op jit(solution)/shard_map/while/body/eval_jaxpr/ppermute | solution.py:17
  329.9 17.4 %collective-permute-start.1 = (f32[2,4,64,128]{2,3,1,0:T(8,128)S(1)}, f32[2,4,64,128]{2,3,1,0:T(8,128)S(1)}, u32[]{:S(2)}, u32[]{:S(2)}) collective-permute-start(f32[2,4,64,128]{2,3,1,0:T(8,128)S(1)} %pad_maximum_fusion.15), channel_id=1, source_target_pairs={{0,2},{2,4},{4,6},{6,8},{8,10},{10,12},{12,14},{14,16},{16,18},{18... | collective-permute-start | bytes 786440 | tf_op jit(solution)/shard_map/while/body/eval_jaxpr/ppermute | solution.py:16
  347.4 4.3 collective-permute-start.2
  350.2 3.1 collective-permute-start.3
  357.9 15.4 %collective-permute-start = (f32[2,4,64,128]{2,3,1,0:T(8,128)S(1)}, f32[2,4,64,128]{2,3,1,0:T(8,128)S(1)}, u32[]{:S(2)}, u32[]{:S(2)}) collective-permute-start(f32[2,4,64,128]{2,3,1,0:T(8,128)S(1)} %pad_maximum_fusion.15), channel_id=1, source_target_pairs={{2,0},{4,2},{6,4},{8,6},{10,8},{12,10},{14,12},{16,14},{18,16},{20... | collective-permute-start | bytes 786440 | tf_op jit(solution)/shard_map/while/body/eval_jaxpr/ppermute | solution.py:17
  359.9 17.4 %collective-permute-start.1 = (f32[2,4,64,128]{2,3,1,0:T(8,128)S(1)}, f32[2,4,64,128]{2,3,1,0:T(8,128)S(1)}, u32[]{:S(2)}, u32[]{:S(2)}) collective-permute-start(f32[2,4,64,128]{2,3,1,0:T(8,128)S(1)} %pad_maximum_fusion.15), channel_id=1, source_target_pairs={{0,2},{2,4},{4,6},{6,8},{8,10},{10,12},{12,14},{14,16},{16,18},{18... | collective-permute-start | bytes 786440 | tf_op jit(solution)/shard_map/while/body/eval_jaxpr/ppermute | solution.py:16
  377.3 4.3 collective-permute-start.2
  380.2 3.1 collective-permute-start.3
  387.9 15.4 %collective-permute-start = (f32[2,4,64,128]{2,3,1,0:T(8,128)S(1)}, f32[2,4,64,128]{2,3,1,0:T(8,128)S(1)}, u32[]{:S(2)}, u32[]{:S(2)}) collective-permute-start(f32[2,4,64,128]{2,3,1,0:T(8,128)S(1)} %pad_maximum_fusion.15), channel_id=1, source_target_pairs={{2,0},{4,2},{6,4},{8,6},{10,8},{12,10},{14,12},{16,14},{18,16},{20... | collective-permute-start | bytes 786440 | tf_op jit(solution)/shard_map/while/body/eval_jaxpr/ppermute | solution.py:17
  389.9 17.4 %collective-permute-start.1 = (f32[2,4,64,128]{2,3,1,0:T(8,128)S(1)}, f32[2,4,64,128]{2,3,1,0:T(8,128)S(1)}, u32[]{:S(2)}, u32[]{:S(2)}) collective-permute-start(f32[2,4,64,128]{2,3,1,0:T(8,128)S(1)} %pad_maximum_fusion.15), channel_id=1, source_target_pairs={{0,2},{2,4},{4,6},{6,8},{8,10},{10,12},{12,14},{14,16},{16,18},{18... | collective-permute-start | bytes 786440 | tf_op jit(solution)/shard_map/while/body/eval_jaxpr/ppermute | solution.py:16
  407.3 4.3 collective-permute-start.2
  410.2 3.1 collective-permute-start.3
  417.8 15.4 %collective-permute-start = (f32[2,4,64,128]{2,3,1,0:T(8,128)S(1)}, f32[2,4,64,128]{2,3,1,0:T(8,128)S(1)}, u32[]{:S(2)}, u32[]{:S(2)}) collective-permute-start(f32[2,4,64,128]{2,3,1,0:T(8,128)S(1)} %pad_maximum_fusion.15), channel_id=1, source_target_pairs={{2,0},{4,2},{6,4},{8,6},{10,8},{12,10},{14,12},{16,14},{18,16},{20... | collective-permute-start | bytes 786440 | tf_op jit(solution)/shard_map/while/body/eval_jaxpr/ppermute | solution.py:17
  419.9 17.4 %collective-permute-start.1 = (f32[2,4,64,128]{2,3,1,0:T(8,128)S(1)}, f32[2,4,64,128]{2,3,1,0:T(8,128)S(1)}, u32[]{:S(2)}, u32[]{:S(2)}) collective-permute-start(f32[2,4,64,128]{2,3,1,0:T(8,128)S(1)} %pad_maximum_fusion.15), channel_id=1, source_target_pairs={{0,2},{2,4},{4,6},{6,8},{8,10},{10,12},{12,14},{14,16},{16,18},{18... | collective-permute-start | bytes 786440 | tf_op jit(solution)/shard_map/while/body/eval_jaxpr/ppermute | solution.py:16
  437.3 4.3 collective-permute-start.2
  440.2 3.1 collective-permute-start.3
  447.8 15.4 %collective-permute-start = (f32[2,4,64,128]{2,3,1,0:T(8,128)S(1)}, f32[2,4,64,128]{2,3,1,0:T(8,128)S(1)}, u32[]{:S(2)}, u32[]{:S(2)}) collective-permute-start(f32[2,4,64,128]{2,3,1,0:T(8,128)S(1)} %pad_maximum_fusion.15), channel_id=1, source_target_pairs={{2,0},{4,2},{6,4},{8,6},{10,8},{12,10},{14,12},{16,14},{18,16},{20... | collective-permute-start | bytes 786440 | tf_op jit(solution)/shard_map/while/body/eval_jaxpr/ppermute | solution.py:17
  449.9 17.4 %collective-permute-start.1 = (f32[2,4,64,128]{2,3,1,0:T(8,128)S(1)}, f32[2,4,64,128]{2,3,1,0:T(8,128)S(1)}, u32[]{:S(2)}, u32[]{:S(2)}) collective-permute-start(f32[2,4,64,128]{2,3,1,0:T(8,128)S(1)} %pad_maximum_fusion.15), channel_id=1, source_target_pairs={{0,2},{2,4},{4,6},{6,8},{8,10},{10,12},{12,14},{14,16},{16,18},{18... | collective-permute-start | bytes 786440 | tf_op jit(solution)/shard_map/while/body/eval_jaxpr/ppermute | solution.py:16
  467.3 4.3 collective-permute-start.2
  470.2 3.1 collective-permute-start.3
  477.8 15.4 %collective-permute-start = (f32[2,4,64,128]{2,3,1,0:T(8,128)S(1)}, f32[2,4,64,128]{2,3,1,0:T(8,128)S(1)}, u32[]{:S(2)}, u32[]{:S(2)}) collective-permute-start(f32[2,4,64,128]{2,3,1,0:T(8,128)S(1)} %pad_maximum_fusion.15), channel_id=1, source_target_pairs={{2,0},{4,2},{6,4},{8,6},{10,8},{12,10},{14,12},{16,14},{18,16},{20... | collective-permute-start | bytes 786440 | tf_op jit(solution)/shard_map/while/body/eval_jaxpr/ppermute | solution.py:17
  479.9 17.4 %collective-permute-start.1 = (f32[2,4,64,128]{2,3,1,0:T(8,128)S(1)}, f32[2,4,64,128]{2,3,1,0:T(8,128)S(1)}, u32[]{:S(2)}, u32[]{:S(2)}) collective-permute-start(f32[2,4,64,128]{2,3,1,0:T(8,128)S(1)} %pad_maximum_fusion.15), channel_id=1, source_target_pairs={{0,2},{2,4},{4,6},{6,8},{8,10},{10,12},{12,14},{14,16},{16,18},{18... | collective-permute-start | bytes 786440 | tf_op jit(solution)/shard_map/while/body/eval_jaxpr/ppermute | solution.py:16
  497.3 4.3 collective-permute-start.2
  500.2 3.1 collective-permute-start.3
  507.8 15.4 %collective-permute-start = (f32[2,4,64,128]{2,3,1,0:T(8,128)S(1)}, f32[2,4,64,128]{2,3,1,0:T(8,128)S(1)}, u32[]{:S(2)}, u32[]{:S(2)}) collective-permute-start(f32[2,4,64,128]{2,3,1,0:T(8,128)S(1)} %pad_maximum_fusion.15), channel_id=1, source_target_pairs={{2,0},{4,2},{6,4},{8,6},{10,8},{12,10},{14,12},{16,14},{18,16},{20... | collective-permute-start | bytes 786440 | tf_op jit(solution)/shard_map/while/body/eval_jaxpr/ppermute | solution.py:17
  509.9 17.4 %collective-permute-start.1 = (f32[2,4,64,128]{2,3,1,0:T(8,128)S(1)}, f32[2,4,64,128]{2,3,1,0:T(8,128)S(1)}, u32[]{:S(2)}, u32[]{:S(2)}) collective-permute-start(f32[2,4,64,128]{2,3,1,0:T(8,128)S(1)} %pad_maximum_fusion.15), channel_id=1, source_target_pairs={{0,2},{2,4},{4,6},{6,8},{8,10},{10,12},{12,14},{14,16},{16,18},{18... | collective-permute-start | bytes 786440 | tf_op jit(solution)/shard_map/while/body/eval_jaxpr/ppermute | solution.py:16
  527.3 4.3 collective-permute-start.2
  537.8 15.4 %collective-permute-start = (f32[2,4,64,128]{2,3,1,0:T(8,128)S(1)}, f32[2,4,64,128]{2,3,1,0:T(8,128)S(1)}, u32[]{:S(2)}, u32[]{:S(2)}) collective-permute-start(f32[2,4,64,128]{2,3,1,0:T(8,128)S(1)} %pad_maximum_fusion.15), channel_id=1, source_target_pairs={{2,0},{4,2},{6,4},{8,6},{10,8},{12,10},{14,12},{16,14},{18,16},{20... | collective-permute-start | bytes 786440 | tf_op jit(solution)/shard_map/while/body/eval_jaxpr/ppermute | solution.py:17
  539.8 17.4 %collective-permute-start.1 = (f32[2,4,64,128]{2,3,1,0:T(8,128)S(1)}, f32[2,4,64,128]{2,3,1,0:T(8,128)S(1)}, u32[]{:S(2)}, u32[]{:S(2)}) collective-permute-start(f32[2,4,64,128]{2,3,1,0:T(8,128)S(1)} %pad_maximum_fusion.15), channel_id=1, source_target_pairs={{0,2},{2,4},{4,6},{6,8},{8,10},{10,12},{12,14},{14,16},{16,18},{18... | collective-permute-start | bytes 786440 | tf_op jit(solution)/shard_map/while/body/eval_jaxpr/ppermute | solution.py:16
  557.3 4.3 collective-permute-start.2
  (25 other events, 494.0 us)
where the time goes:
time: 668 us; the launch traced here: 660 us
  waiting for transfers between devices  303 us (45%)
  starting transfers between devices  182 us (27%)
  blocking collectives  90.4 us (14%)
  other arithmetic  43.8 us (7%)
  local copies, waits for them, and re-layouts  38.8 us (6%)
    ppermute x34, waiting for transfers between devices, padded(): after = lax.ppermute(leading, axis, down)  160 us
    ppermute x34, waiting for transfers between devices, padded(): before = lax.ppermute(last, axis, up)  143 us
    all_to_all x1, blocking collectives, per_device(): return lax.all_to_all(result, 'tm', split_axis=0, concat_axis=1, tiled=True)  90.4 us
    ppermute x34, starting transfers between devices, padded(): after = lax.ppermute(leading, axis, down)  89.5 us
    ppermute x34, starting transfers between devices, padded(): before = lax.ppermute(last, axis, up)  77.7 us
    div x64, other arithmetic, relax_cells(): (source + diffus * beside + drift_rate * upstream) / (1.0 + 6.0 * diffus...  36.2 us
    dynamic_slice x32, local copies, waits for them, and re-layouts, per_device(): final, result = lax.scan(advance, initial, slabs)  16.7 us
    all_to_all x1, starting transfers between devices, per_device(): lax.all_to_all(forcing, 'tm', split_axis=1, concat_axis=0, tiled=True)  15.3 us
  transfers between devices with their start and end apart: 69, of which 50 were waited for; matrix products, arithmetic and copies ran while one was open for 1% of the time, Pallas kernels for 0%

commit v1 on v0

v1 whole, which is shorter than its diff:
```python
import jax
import jax.numpy as jnp
from jax import lax
from jax.experimental import pallas as pl
from jax.experimental.pallas import tpu as pltpu
from jax.sharding import PartitionSpec as P

NT = 16
COLS = 16
RING = 8
LEAD = 6
MESH = pl.DeviceIdType.MESH
F32 = jnp.float32


def remote(src, dst, send, recv, device):
    return pltpu.make_async_remote_copy(
        src_ref=src, dst_ref=dst, send_sem=send, recv_sem=recv, device_id=device, device_id_type=MESH
    )


def await_bytes(ref, sem):
    pltpu.make_async_copy(ref, ref, sem).wait()


def kernel(
    forcing, initial, diffusion, drift, out,
    F, G, O, E, C, D, R, DP, EP, IV, SP, W1, W2,
    csend, crecv, xsend, xrecv, fsend, frecv, gsend, grecv, hsend, hrecv, osend, orecv,
):
    t = lax.axis_index("tm")
    c = lax.axis_index("space")
    q = t // RING
    j = t % RING
    part = 2 * q + c

    def plane_device(p):
        return ((p // 2) * RING + j, p % 2)

    barrier = pltpu.get_barrier_semaphore()

    def greet(device):
        pl.semaphore_signal(barrier, inc=1, device_id=device, device_id_type=MESH)

    @pl.loop(1, 2 * COLS)
    def _(n):
        greet(plane_device((part + n) % (2 * COLS)))

    @pl.loop(1, RING)
    def _(n):
        chip = q * RING + (j + n) % RING
        greet((chip, c))
        greet((chip, 1 - c))

    beyond = (q + COLS - 1 + 2 * c) % COLS
    left, right = (j + RING - 1) % RING, (j + 1) % RING
    greet((beyond * RING + left, 1 - c))
    greet((beyond * RING + right, 1 - c))
    pl.semaphore_wait(barrier, (2 * COLS - 1) + 2 * (RING - 1) + 2)

    up = (part + 1) % (2 * COLS)
    down = (part + 2 * COLS - 1) % (2 * COLS)

    def at(p, jj):
        return ((p // 2) * RING + jj, p % 2)

    lower = pl.ds(4, 4)
    upper = pl.ds(0, 4)

    def halo_copies(A, send, recv):
        lo, hi = pl.ds(4, 4), pl.ds(16, 4)
        own = pl.ds(4, 16)
        below, above = pl.ds(0, 4), pl.ds(20, 4)
        moves = [
            (own, 0, lower, own, 1, part, left),
            (own, 1, upper, own, 0, part, right),
            (hi, 0, lower, below, 1, up, left),
            (hi, 1, upper, below, 0, up, right),
            (lo, 0, lower, above, 1, down, left),
            (lo, 1, upper, above, 0, down, right),
            (hi, 0, lower, below, 0, up, j),
            (hi, 1, upper, below, 1, up, j),
            (lo, 0, lower, above, 0, down, j),
            (lo, 1, upper, above, 1, down, j),
        ]
        for zs, tile, rows, zd, tiled, p, jj in moves:
            remote(
                A.at[zs, tile, :, rows, :], A.at[zd, tiled, :, rows, :], send, recv, at(p, jj)
            ).start()

    half = j // 4
    zs = pl.ds((j % 4) * 4, 4)
    stay = c == half
    for n in range(RING):
        jj = (j + n) % RING
        for a, ref in enumerate((initial, diffusion, drift)):
            src = ref.at[:, pl.ds(pl.multiple_of(jj * 8, 8), 8), :]
            dst = C.at[a, c, zs]
            if n == 0:
                @pl.when(stay)
                def _():
                    pltpu.make_async_copy(src, dst, crecv).start()

                @pl.when(jnp.logical_not(stay))
                def _():
                    remote(src, dst, csend, crecv, (t, 1 - c)).start()
            else:
                remote(src, dst, csend, crecv, (q * RING + jj, half)).start()

    def send_forcing(first, last):
        @pl.loop(first, last)
        def _(n):
            p = (part + n) % (2 * COLS)
            remote(
                forcing.at[0, pl.ds(p * 16, 16)], F.at[2 * q + c], fsend, frecv.at[q], plane_device(p)
            ).start()

    def keep_forcing():
        pltpu.make_async_copy(forcing.at[0, pl.ds(part * 16, 16)], F.at[2 * q + c], frecv.at[q]).start()

    @pl.when(q < LEAD)
    def _():
        keep_forcing()
        send_forcing(1, 2 * COLS)

    def place(A, h, v):
        A[pl.ds(4, 16), 0, h, pl.ds(4, 4), :] = v[:, 0:4, :]
        A[pl.ds(4, 16), 1, h, pl.ds(0, 4), :] = v[:, 4:8, :]

    await_bytes(C, crecv)
    for h in range(2):
        place(D, h, C[1, h])
        place(R, h, C[2, h])
    halo_copies(D, xsend, xrecv)
    halo_copies(R, xsend, xrecv)
    for h in range(2):
        place(E.at[0], h, C[0, h])
    halo_copies(E.at[0], hsend.at[0], hrecv.at[0])

    def prepare_force(k):
        await_bytes(F.at[pl.ds(2 * k, 2)], frecv.at[k])
        for h in range(2):
            place(G.at[k], h, F[2 * k + h])
        halo_copies(G.at[k], gsend, grecv.at[k])

    def clear_outside(A):
        @pl.when(part == 0)
        def _():
            A[pl.ds(0, 4)] = jnp.zeros((4, 2, 2, 8, 128), F32)

        @pl.when(part == 2 * COLS - 1)
        def _():
            A[pl.ds(20, 4)] = jnp.zeros((4, 2, 2, 8, 128), F32)

        @pl.when(j == 0)
        def _():
            A[:, 0, :, pl.ds(0, 4), :] = jnp.zeros((24, 2, 4, 128), F32)

        @pl.when(j == RING - 1)
        def _():
            A[:, 1, :, pl.ds(4, 4), :] = jnp.zeros((24, 2, 4, 128), F32)

    await_bytes(G.at[pl.ds(0, 2), pl.ds(0, 16)], xrecv)
    for z in range(0, 24, 4):
        s = pl.ds(z, 4)
        d, r = D[s], R[s]
        inv = 1.0 / (1.0 + 6.0 * d + r)
        IV[s] = inv
        DP[s] = d * inv
        EP[s] = (d + r) * inv
    for A in (IV, DP, EP):
        clear_outside(A)

    prepare_force(0)
    prepare_force(1)

    def relax(load, load_s, z, n):
        shape = (n, 8, 128)
        row = lax.broadcasted_iota(jnp.int32, shape, 1)
        lane = lax.broadcasted_iota(jnp.int32, shape, 2)
        first_row, last_row = row == 0, row == 7
        first_lane, last_lane = lane == 0, lane == 127
        zero = jnp.zeros(shape, F32)
        wide = [[load(z - 1, n + 2, T, h) for h in range(2)] for T in range(2)]
        mid = [[wide[T][h][1:-1] for h in range(2)] for T in range(2)]
        result = [[None, None], [None, None]]
        beside = [[None, None], [None, None]]
        for h in range(2):
            a0, a1 = pltpu.roll(mid[0][h], 1, 1), pltpu.roll(mid[1][h], 1, 1)
            b0, b1 = pltpu.roll(mid[0][h], 7, 1), pltpu.roll(mid[1][h], 7, 1)
            beside[0][h] = a0 + jnp.where(last_row, b1, b0)
            beside[1][h] = jnp.where(first_row, a0, a1) + b1
        for T in range(2):
            a0, a1 = pltpu.roll(mid[T][0], 1, 2), pltpu.roll(mid[T][1], 1, 2)
            b0, b1 = pltpu.roll(mid[T][0], 127, 2), pltpu.roll(mid[T][1], 127, 2)
            across = (
                jnp.where(first_lane, zero, a0) + jnp.where(last_lane, b1, b0),
                jnp.where(first_lane, a0, a1) + jnp.where(last_lane, zero, b1),
            )
            for h in range(2):
                total = beside[T][h] + across[h] + wide[T][h][2:]
                s = pl.ds(z, n)
                result[T][h] = (
                    load_s(z, n, T, h) + DP[s, T, h] * total + EP[s, T, h] * wide[T][h][:-2]
                )
        return result

    def chunks(first, last):
        z = first
        while z < last:
            n = min(4, last - z)
            yield z, n
            z += n

    def from_ref(A):
        return lambda z, n, T, h: A[pl.ds(z, n), T, h]

    @pl.loop(0, NT)
    def _(k):
        par = k % 2
        now, later = E.at[par], E.at[1 - par]
        force = G.at[k]
        await_bytes(G.at[0, pl.ds(0, 16)], hrecv.at[par])
        await_bytes(G.at[0, pl.ds(0, 16)], grecv.at[k])
        clear_outside(now)

        def make_source(z, n, T, h):
            s = pl.ds(z, n)
            v = (now[s, T, h] + force[s, T, h]) * IV[s, T, h]
            SP[s, T, h] = v
            return v

        for load, load_s, W, margin in (
            (from_ref(now), make_source, W1, 1),
            (from_ref(W1), from_ref(SP), W2, 2),
            (from_ref(W2), from_ref(SP), W1, 3),
        ):
            for z, n in chunks(margin, 24 - margin):
                v = relax(load, load_s, z, n)
                for T in range(2):
                    for h in range(2):
                        W[pl.ds(z, n), T, h] = v[T][h]

        @pl.when(k > 0)
        def _():
            await_bytes(G.at[0, pl.ds(0, 16)], hsend.at[1 - par])

        for z, n in chunks(4, 20):
            v = relax(from_ref(W1), from_ref(SP), z, n)
            row = lax.broadcasted_iota(jnp.int32, (n, 8, 128), 1)
            for h in range(2):
                later[pl.ds(z, n), 0, h, pl.ds(4, 4), :] = v[0][h][:, 4:8, :]
                later[pl.ds(z, n), 1, h, pl.ds(0, 4), :] = v[1][h][:, 0:4, :]
                O[k, h, pl.ds(z - 4, n)] = jnp.where(
                    row < 4, pltpu.roll(v[0][h], 4, 1), pltpu.roll(v[1][h], 4, 1)
                )

        @pl.when(k < NT - 1)
        def _():
            halo_copies(later, hsend.at[1 - par], hrecv.at[1 - par])

        for h in range(2):
            src, dst = O.at[k, h], out.at[0, pl.ds(part * 16, 16)]
            mine = jnp.logical_and(k == q, c == h)

            @pl.when(mine)
            def _():
                pltpu.make_async_copy(src, dst, orecv).start()

            @pl.when(jnp.logical_not(mine))
            def _():
                remote(src, dst, osend, orecv, (k * RING + j, h)).start()

        @pl.when(q - LEAD == k)
        def _():
            keep_forcing()
            send_forcing(1, COLS)

        @pl.when(q - LEAD + 1 == k)
        def _():
            @pl.when(q >= LEAD)
            def _():
                send_forcing(COLS, 2 * COLS)

        @pl.when(k < NT - 2)
        def _():
            prepare_force(k + 2)

    @pl.when(stay)
    def _():
        await_bytes(F.at[pl.ds(0, 6), pl.ds(0, 14)], csend)

    @pl.when(jnp.logical_not(stay))
    def _():
        await_bytes(C, csend)

    await_bytes(G.at[pl.ds(0, 2), pl.ds(0, 16)], xsend)
    await_bytes(G.at[0, pl.ds(0, 16)], hsend.at[1])
    await_bytes(G.at[:, pl.ds(0, 16)], gsend)
    await_bytes(F.at[pl.ds(0, 31)], fsend)
    await_bytes(F.at[pl.ds(0, 31)], osend)
    await_bytes(out, orecv)


def per_device(forcing, initial, diffusion, drift):
    wide = (24, 2, 2, 8, 128)
    vmem = lambda *shape: pltpu.VMEM(shape, F32)
    dma = pltpu.SemaphoreType.DMA
    return pl.pallas_call(
        kernel,
        out_shape=jax.ShapeDtypeStruct(forcing.shape, F32),
        in_specs=[pl.BlockSpec(memory_space=pl.ANY)] * 4,
        out_specs=pl.BlockSpec(memory_space=pl.ANY),
        scratch_shapes=[
            vmem(2 * NT, 16, 8, 128),
            vmem(NT, *wide),
            vmem(NT, 2, 16, 8, 128),
            vmem(2, *wide),
            vmem(3, 2, 16, 8, 128),
        ]
        + [vmem(*wide)] * 8
        + [dma, dma, dma, dma, dma, dma((NT,)), dma, dma((NT,)), dma((2,)), dma((2,)), dma, dma],
        compiler_params=pltpu.CompilerParams(
            collective_id=0, has_side_effects=True, vmem_limit_bytes=40 * 1024 * 1024
        ),
    )(forcing, initial, diffusion, drift)


def solution(mesh):
    in_specs = (
        P("tm", None, None, "space"),
        P("tm", None, "space"),
        P("tm", None, "space"),
        P("tm", None, "space"),
    )
    out_specs = P("tm", None, None, "space")
    return jax.shard_map(
        per_device, mesh=mesh, in_specs=in_specs, out_specs=out_specs, check_vma=False
    )
```

time: 668 us -> 187 us (0.28); the launches traced: 660 us -> 187 us
  waiting for transfers between devices: 303 us -> 0 us
  Pallas kernels: 0 us -> 182 us
  starting transfers between devices: 182 us -> 0 us
  blocking collectives: 90.4 us -> 0 us
  other arithmetic: 43.8 us -> 0 us
  local copies, waits for them, and re-layouts: 38.8 us -> 5.62 us
    ppermute x68 -> x0, waiting for transfers between devices: 303 us -> none  [the longest x34 160 us: padded(): after = lax.ppermute(leading, axis, down)]
    pallas_call x0 -> x1, Pallas kernels: none -> 182 us  [per_device(): pl.pallas_call(kernel, out_shape=jax.ShapeDtypeStruct(forcing.shape, F32)...]
    ppermute x68 -> x0, starting transfers between devices: 167 us -> none  [the longest x34 89.5 us: padded(): after = lax.ppermute(leading, axis, down)]
    all_to_all x1 -> x0, blocking collectives: 90.4 us -> none  [per_device(): return lax.all_to_all(result, 'tm', split_axis=0, concat_axis=1, tiled=True)]
    div x64 -> x0, other arithmetic: 36.2 us -> none  [relax_cells(): (source + diffus * beside + drift_rate * upstream) / (1.0 + 6.0 * diffus...]
    dynamic_slice x32 -> x0, local copies, waits for them, and re-layouts: 16.7 us -> none  [per_device(): final, result = lax.scan(advance, initial, slabs)]
    all_to_all x1 -> x0, starting transfers between devices: 15.3 us -> none  [per_device(): lax.all_to_all(forcing, 'tm', split_axis=1, concat_axis=0, tiled=True)]
    dynamic_update_slice x32 -> x0, local copies, waits for them, and re-layouts: 12.5 us -> none  [per_device(): final, result = lax.scan(advance, initial, slabs)]
  transfers between devices with their start and end apart: 69 -> 0, of which waited for: 50 -> 0; matrix products, arithmetic and copies ran while one was open for 1% -> 0% of each run, Pallas kernels for 0% -> 0%
where the time goes in v1:
time: 187 us
  Pallas kernels  182 us (97%)
  local copies, waits for them, and re-layouts  5.62 us (3%)
    pallas_call x1, Pallas kernels, per_device(): pl.pallas_call(kernel, out_shape=jax.ShapeDtypeStruct(forcing.shape, F32)...  182 us
    unnamed x9, local copies, waits for them, and re-layouts  5.62 us

profile of v1, /device:TPU:31, one launch (start us, length us, event | category | flops | bytes accessed | tf_op | source)
XLA Modules:
  0.0 187.2 jit_solution(14011380936849994170)
XLA Ops:
  0.0 0.0 copy-start
  0.0 1.6 copy-done
  1.6 0.0 copy-start.1
  1.6 0.9 copy-done.1
  2.5 0.0 copy-start.2
  2.5 0.9 copy-done.2
  3.4 0.0 copy-start.3
  3.4 0.9 copy-done.3
  4.3 181.5 %shard_map.46 = f32[1,512,8,128]{3,2,1,0:T(8,128)S(1)} custom-call(f32[1,512,8,128]{3,2,1,0:T(8,128)S(1)} %copy-done, f32[4,64,128]{2,1,0:T(8,128)S(1)} %copy-done.1, f32[4,64,128]{2,1,0:T(8,128)S(1)} %copy-done.2, f32[4,64,128]{2,1,0:T(8,128)S(1)} %copy-done.3), custom_call_target="tpu_custom_call" | custom-call | tf_op jit(solution)/shard_map/pallas_call | solution.py:309
  185.8 1.3 copy.6
Async XLA Ops:
  0.0 1.6 copy-start
  1.6 0.9 copy-start.1
  2.5 0.9 copy-start.2
  3.4 0.9 copy-start.3

commit v2 on v1

--- a/solution.py
+++ b/solution.py
@@ -11,6 +11,11 @@
 LEAD = 6
 MESH = pl.DeviceIdType.MESH
 F32 = jnp.float32
+
+
+def snake(n):
+    y, x = n // 4, n % 4
+    return y * 4 + x + (y % 2) * (3 - 2 * x)
 
 
 def remote(src, dst, send, recv, device):
@@ -32,10 +37,13 @@
     c = lax.axis_index("space")
     q = t // RING
     j = t % RING
-    part = 2 * q + c
+    part = 2 * snake(q) + c
+
+    def at(p, jj):
+        return (snake(p // 2) * RING + jj, p % 2)
 
     def plane_device(p):
-        return ((p // 2) * RING + j, p % 2)
+        return at(p, j)
 
     barrier = pltpu.get_barrier_semaphore()
 
@@ -48,21 +56,22 @@
 
     @pl.loop(1, RING)
     def _(n):
-        chip = q * RING + (j + n) % RING
+        chip = snake(q) * RING + (j + n) % RING
         greet((chip, c))
         greet((chip, 1 - c))
 
-    beyond = (q + COLS - 1 + 2 * c) % COLS
     left, right = (j + RING - 1) % RING, (j + 1) % RING
-    greet((beyond * RING + left, 1 - c))
-    greet((beyond * RING + right, 1 - c))
-    pl.semaphore_wait(barrier, (2 * COLS - 1) + 2 * (RING - 1) + 2)
-
     up = (part + 1) % (2 * COLS)
     down = (part + 2 * COLS - 1) % (2 * COLS)
-
-    def at(p, jj):
-        return ((p // 2) * RING + jj, p % 2)
+    for jj in (left, right):
+        for p in (part, up, down):
+            greet(at(p, jj))
+    pl.semaphore_wait(barrier, (2 * COLS - 1) + 2 * (RING - 1) + 6)
+
+    has_left, has_right = j > 0, j < RING - 1
+    has_down, has_up = part > 0, part < 2 * COLS - 1
+    x_edge = jnp.logical_or(j == 0, j == RING - 1)
+    z_edge = jnp.logical_or(part == 0, part == 2 * COLS - 1)
 
     lower = pl.ds(4, 4)
     upper = pl.ds(0, 4)
@@ -71,26 +80,57 @@
         lo, hi = pl.ds(4, 4), pl.ds(16, 4)
         own = pl.ds(4, 16)
         below, above = pl.ds(0, 4), pl.ds(20, 4)
-        moves = [
-            (own, 0, lower, own, 1, part, left),
-            (own, 1, upper, own, 0, part, right),
-            (hi, 0, lower, below, 1, up, left),
-            (hi, 1, upper, below, 0, up, right),
-            (lo, 0, lower, above, 1, down, left),
-            (lo, 1, upper, above, 0, down, right),
-            (hi, 0, lower, below, 0, up, j),
-            (hi, 1, upper, below, 1, up, j),
-            (lo, 0, lower, above, 0, down, j),
-            (lo, 1, upper, above, 1, down, j),
-        ]
-        for zs, tile, rows, zd, tiled, p, jj in moves:
+
+        def move(zs, tile, rows, zd, tiled, p, jj, group):
             remote(
-                A.at[zs, tile, :, rows, :], A.at[zd, tiled, :, rows, :], send, recv, at(p, jj)
+                A.at[zs, tile, :, rows, :], A.at[zd, tiled, :, rows, :],
+                send.at[group], recv.at[group], at(p, jj),
             ).start()
+
+        for has_z, zs, zd, p in ((has_up, hi, below, up), (has_down, lo, above, down)):
+            @pl.when(jnp.logical_and(has_z, has_left))
+            def _():
+                move(zs, 0, lower, zd, 1, p, left, 2)
+
+            @pl.when(jnp.logical_and(has_z, has_right))
+            def _():
+                move(zs, 1, upper, zd, 0, p, right, 2)
+
+        @pl.when(has_left)
+        def _():
+            move(own, 0, lower, own, 1, part, left, 0)
+
+        @pl.when(has_right)
+        def _():
+            move(own, 1, upper, own, 0, part, right, 0)
+
+        for has_z, zs, zd, p in ((has_up, hi, below, up), (has_down, lo, above, down)):
+            @pl.when(has_z)
+            def _():
+                move(zs, 0, lower, zd, 0, p, j, 1)
+                move(zs, 1, upper, zd, 1, p, j, 1)
+
+    def await_halos(sem):
+        inside = jnp.logical_not
+
+        def await_tiles(condition, group, n):
+            @pl.when(condition)
+            def _():
+                await_bytes(G.at[0, pl.ds(0, n // 4)], sem.at[group])
+
+        await_tiles(inside(x_edge), 0, 32)
+        await_tiles(x_edge, 0, 16)
+        await_tiles(inside(z_edge), 1, 16)
+        await_tiles(z_edge, 1, 8)
+        await_tiles(jnp.logical_and(inside(z_edge), inside(x_edge)), 2, 16)
+        await_tiles(jnp.logical_and(z_edge, inside(x_edge)), 2, 8)
+        await_tiles(jnp.logical_and(inside(z_edge), x_edge), 2, 8)
+        await_tiles(jnp.logical_and(z_edge, x_edge), 2, 4)
 
     half = j // 4
     zs = pl.ds((j % 4) * 4, 4)
-    stay = c == half
+    home = snake(q) == q
+    stay = jnp.logical_and(c == half, home)
     for n in range(RING):
         jj = (j + n) % RING
         for a, ref in enumerate((initial, diffusion, drift)):
@@ -103,9 +143,9 @@
 
                 @pl.when(jnp.logical_not(stay))
                 def _():
-                    remote(src, dst, csend, crecv, (t, 1 - c)).start()
+                    remote(src, dst, csend, crecv, (snake(q) * RING + j, half)).start()
             else:
-                remote(src, dst, csend, crecv, (q * RING + jj, half)).start()
+                remote(src, dst, csend, crecv, (snake(q) * RING + jj, half)).start()
 
     def send_forcing(first, last):
         @pl.loop(first, last)
@@ -127,40 +167,44 @@
         A[pl.ds(4, 16), 0, h, pl.ds(4, 4), :] = v[:, 0:4, :]
         A[pl.ds(4, 16), 1, h, pl.ds(0, 4), :] = v[:, 4:8, :]
 
+    def clear_outside(A):
+        @pl.when(part == 0)
+        def _():
+            A[pl.ds(0, 4)] = jnp.zeros((4, 2, 2, 8, 128), F32)
+
+        @pl.when(part == 2 * COLS - 1)
+        def _():
+            A[pl.ds(20, 4)] = jnp.zeros((4, 2, 2, 8, 128), F32)
+
+        @pl.when(j == 0)
+        def _():
+            A[:, 0, :, pl.ds(0, 4), :] = jnp.zeros((24, 2, 4, 128), F32)
+
+        @pl.when(j == RING - 1)
+        def _():
+            A[:, 1, :, pl.ds(4, 4), :] = jnp.zeros((24, 2, 4, 128), F32)
+
+    clear_outside(E.at[0])
+    clear_outside(E.at[1])
     await_bytes(C, crecv)
     for h in range(2):
         place(D, h, C[1, h])
         place(R, h, C[2, h])
-    halo_copies(D, xsend, xrecv)
-    halo_copies(R, xsend, xrecv)
+    halo_copies(D, xsend.at[0], xrecv.at[0])
+    halo_copies(R, xsend.at[1], xrecv.at[1])
     for h in range(2):
         place(E.at[0], h, C[0, h])
     halo_copies(E.at[0], hsend.at[0], hrecv.at[0])
 
     def prepare_force(k):
         await_bytes(F.at[pl.ds(2 * k, 2)], frecv.at[k])
+        clear_outside(G.at[k])
         for h in range(2):
             place(G.at[k], h, F[2 * k + h])
-        halo_copies(G.at[k], gsend, grecv.at[k])
-
-    def clear_outside(A):
-        @pl.when(part == 0)
-        def _():
-            A[pl.ds(0, 4)] = jnp.zeros((4, 2, 2, 8, 128), F32)
-
-        @pl.when(part == 2 * COLS - 1)
-        def _():
-            A[pl.ds(20, 4)] = jnp.zeros((4, 2, 2, 8, 128), F32)
-
-        @pl.when(j == 0)
-        def _():
-            A[:, 0, :, pl.ds(0, 4), :] = jnp.zeros((24, 2, 4, 128), F32)
-
-        @pl.when(j == RING - 1)
-        def _():
-            A[:, 1, :, pl.ds(4, 4), :] = jnp.zeros((24, 2, 4, 128), F32)
-
-    await_bytes(G.at[pl.ds(0, 2), pl.ds(0, 16)], xrecv)
+        halo_copies(G.at[k], gsend.at[k], grecv.at[k])
+
+    await_halos(xrecv.at[0])
+    await_halos(xrecv.at[1])
     for z in range(0, 24, 4):
         s = pl.ds(z, 4)
         d, r = D[s], R[s]
@@ -220,9 +264,8 @@
         par = k % 2
         now, later = E.at[par], E.at[1 - par]
         force = G.at[k]
-        await_bytes(G.at[0, pl.ds(0, 16)], hrecv.at[par])
-        await_bytes(G.at[0, pl.ds(0, 16)], grecv.at[k])
-        clear_outside(now)
+        await_halos(hrecv.at[par])
+        await_halos(grecv.at[k])
 
         def make_source(z, n, T, h):
             s = pl.ds(z, n)
@@ -243,7 +286,7 @@
 
         @pl.when(k > 0)
         def _():
-            await_bytes(G.at[0, pl.ds(0, 16)], hsend.at[1 - par])
+            await_halos(hsend.at[1 - par])
 
         for z, n in chunks(4, 20):
             v = relax(from_ref(W1), from_ref(SP), z, n)
@@ -294,9 +337,14 @@
     def _():
         await_bytes(C, csend)
 
-    await_bytes(G.at[pl.ds(0, 2), pl.ds(0, 16)], xsend)
-    await_bytes(G.at[0, pl.ds(0, 16)], hsend.at[1])
-    await_bytes(G.at[:, pl.ds(0, 16)], gsend)
+    await_halos(xsend.at[0])
+    await_halos(xsend.at[1])
+    await_halos(hsend.at[1])
+
+    @pl.loop(0, NT)
+    def _(k):
+        await_halos(gsend.at[k])
+
     await_bytes(F.at[pl.ds(0, 31)], fsend)
     await_bytes(F.at[pl.ds(0, 31)], osend)
     await_bytes(out, orecv)
@@ -309,7 +357,7 @@
     return pl.pallas_call(
         kernel,
         out_shape=jax.ShapeDtypeStruct(forcing.shape, F32),
-        in_specs=[pl.BlockSpec(memory_space=pl.ANY)] * 4,
+        in_specs=[pl.BlockSpec(memory_space=pltpu.HBM)] * 4,
         out_specs=pl.BlockSpec(memory_space=pl.ANY),
         scratch_shapes=[
             vmem(2 * NT, 16, 8, 128),
@@ -319,9 +367,10 @@
             vmem(3, 2, 16, 8, 128),
         ]
         + [vmem(*wide)] * 8
-        + [dma, dma, dma, dma, dma, dma((NT,)), dma, dma((NT,)), dma((2,)), dma((2,)), dma, dma],
+        + [dma, dma, dma((2, 3)), dma((2, 3)), dma, dma((NT,)), dma((NT, 3)), dma((NT, 3))]
+        + [dma((2, 3)), dma((2, 3)), dma, dma],
         compiler_params=pltpu.CompilerParams(
-            collective_id=0, has_side_effects=True, vmem_limit_bytes=40 * 1024 * 1024
+            collective_id=0, has_side_effects=True, vmem_limit_bytes=60 * 1024 * 1024
         ),
     )(forcing, initial, diffusion, drift)
 

time: 187 us -> 176 us (0.941)
  Pallas kernels: 182 us -> 172 us
  local copies, waits for them, and re-layouts: 5.62 us -> 3.05 us
    pallas_call x1, Pallas kernels: 182 us -> 172 us  [per_device(): pl.pallas_call(kernel, out_shape=jax.ShapeDtypeStruct(forcing.shape, F32)...]
    unnamed x9 -> x1, local copies, waits for them, and re-layouts: 5.62 us -> 3.05 us
where the time goes in v2:
time: 176 us; the launch traced here: 175 us
  Pallas kernels  172 us (98%)
  local copies, waits for them, and re-layouts  3.05 us (2%)
    pallas_call x1, Pallas kernels, per_device(): pl.pallas_call(kernel, out_shape=jax.ShapeDtypeStruct(forcing.shape, F32)...  172 us

profile of v2, /device:TPU:31, one launch (start us, length us, event | category | flops | bytes accessed | tf_op | source)
XLA Modules:
  0.0 175.4 jit_solution(9957467978981925834)
XLA Ops:
  0.0 172.3 %shard_map.46 = f32[1,512,8,128]{3,2,1,0:T(8,128)} custom-call(f32[1,512,8,128]{3,2,1,0:T(8,128)} %forcing.1, f32[4,64,128]{2,1,0:T(8,128)} %initial.1, f32[4,64,128]{2,1,0:T(8,128)} %diffusion.1, f32[4,64,128]{2,1,0:T(8,128)} %drift.1), custom_call_target="tpu_custom_call" | custom-call | tf_op jit(solution)/shard_map/pallas_call | solution.py:357
  172.3 3.0 %copy.6 = f32[1,512,8,128]{3,2,1,0:T(8,128)} copy(f32[1,512,8,128]{3,2,1,0:T(8,128)} %shard_map.46) | data formatting | bytes 4194304

commit v3 on v2

--- a/solution.py
+++ b/solution.py
@@ -8,7 +8,8 @@
 NT = 16
 COLS = 16
 RING = 8
-LEAD = 6
+FIRST = 3
+PIECES = 4
 MESH = pl.DeviceIdType.MESH
 F32 = jnp.float32
 
@@ -158,7 +159,7 @@
     def keep_forcing():
         pltpu.make_async_copy(forcing.at[0, pl.ds(part * 16, 16)], F.at[2 * q + c], frecv.at[q]).start()
 
-    @pl.when(q < LEAD)
+    @pl.when(q < FIRST)
     def _():
         keep_forcing()
         send_forcing(1, 2 * COLS)
@@ -201,6 +202,8 @@
         clear_outside(G.at[k])
         for h in range(2):
             place(G.at[k], h, F[2 * k + h])
+
+    def send_force(k):
         halo_copies(G.at[k], gsend.at[k], grecv.at[k])
 
     await_halos(xrecv.at[0])
@@ -216,7 +219,13 @@
         clear_outside(A)
 
     prepare_force(0)
-    prepare_force(1)
+    send_force(0)
+    await_halos(hsend.at[0])
+
+    @pl.when(q >= FIRST)
+    def _():
+        keep_forcing()
+        send_forcing(1, 2 * COLS)
 
     def relax(load, load_s, z, n):
         shape = (n, 8, 128)
@@ -259,6 +268,21 @@
     def from_ref(A):
         return lambda z, n, T, h: A[pl.ds(z, n), T, h]
 
+    def send_state(k, piece):
+        rows = 16 // PIECES
+        for h in range(2):
+            src = O.at[k, h, pl.ds(piece * rows, rows)]
+            dst = out.at[0, pl.ds(part * 16 + piece * rows, rows)]
+            mine = jnp.logical_and(k == q, c == h)
+
+            @pl.when(mine)
+            def _():
+                pltpu.make_async_copy(src, dst, orecv).start()
+
+            @pl.when(jnp.logical_not(mine))
+            def _():
+                remote(src, dst, osend, orecv, (k * RING + j, h)).start()
+
     @pl.loop(0, NT)
     def _(k):
         par = k % 2
@@ -266,6 +290,7 @@
         force = G.at[k]
         await_halos(hrecv.at[par])
         await_halos(grecv.at[k])
+
 
         def make_source(z, n, T, h):
             s = pl.ds(z, n)
@@ -284,10 +309,6 @@
                     for h in range(2):
                         W[pl.ds(z, n), T, h] = v[T][h]
 
-        @pl.when(k > 0)
-        def _():
-            await_halos(hsend.at[1 - par])
-
         for z, n in chunks(4, 20):
             v = relax(from_ref(W1), from_ref(SP), z, n)
             row = lax.broadcasted_iota(jnp.int32, (n, 8, 128), 1)
@@ -302,32 +323,34 @@
         def _():
             halo_copies(later, hsend.at[1 - par], hrecv.at[1 - par])
 
-        for h in range(2):
-            src, dst = O.at[k, h], out.at[0, pl.ds(part * 16, 16)]
-            mine = jnp.logical_and(k == q, c == h)
-
-            @pl.when(mine)
-            def _():
-                pltpu.make_async_copy(src, dst, orecv).start()
-
-            @pl.when(jnp.logical_not(mine))
-            def _():
-                remote(src, dst, osend, orecv, (k * RING + j, h)).start()
-
-        @pl.when(q - LEAD == k)
-        def _():
-            keep_forcing()
-            send_forcing(1, COLS)
-
-        @pl.when(q - LEAD + 1 == k)
-        def _():
-            @pl.when(q >= LEAD)
-            def _():
-                send_forcing(COLS, 2 * COLS)
+        for d in range(PIECES):
+            @pl.when(k >= d)
+            def _():
+                send_state(k - d, d)
+
+        @pl.when(k == 0)
+        def _():
+            prepare_force(1)
 
         @pl.when(k < NT - 2)
         def _():
             prepare_force(k + 2)
+
+        @pl.when(k < NT - 1)
+        def _():
+            await_halos(hsend.at[1 - par])
+
+        @pl.when(k == 0)
+        def _():
+            send_force(1)
+
+        @pl.when(k < NT - 2)
+        def _():
+            send_force(k + 2)
+
+    for k in range(NT - PIECES + 1, NT):
+        for piece in range(NT - k, PIECES):
+            send_state(k, piece)
 
     @pl.when(stay)
     def _():
@@ -339,7 +362,6 @@
 
     await_halos(xsend.at[0])
     await_halos(xsend.at[1])
-    await_halos(hsend.at[1])
 
     @pl.loop(0, NT)
     def _(k):
@@ -370,9 +392,9 @@
         + [dma, dma, dma((2, 3)), dma((2, 3)), dma, dma((NT,)), dma((NT, 3)), dma((NT, 3))]
         + [dma((2, 3)), dma((2, 3)), dma, dma],
         compiler_params=pltpu.CompilerParams(
-            collective_id=0, has_side_effects=True, vmem_limit_bytes=60 * 1024 * 1024
+            collective_id=0, has_side_effects=True, vmem_limit_bytes=40 * 1024 * 1024
         ),
-    )(forcing, initial, diffusion, drift)
+    )(*[pltpu.with_memory_space_constraint(a, pltpu.HBM) for a in (forcing, initial, diffusion, drift)])
 
 
 def solution(mesh):

time: 176 us -> 162 us (0.920)
  Pallas kernels: 172 us -> 161 us
    pallas_call x1, Pallas kernels: 172 us -> 161 us  [per_device(): pl.pallas_call(kernel, out_shape=jax.ShapeDtypeStruct(forcing.shape, F32)...]
where the time goes in v3:
time: 162 us
  Pallas kernels  161 us (99%)
    pallas_call x1, Pallas kernels, per_device(): pl.pallas_call(kernel, out_shape=jax.ShapeDtypeStruct(forcing.shape, F32)...  161 us

profile of v3, /device:TPU:31, one launch (start us, length us, event | category | flops | bytes accessed | tf_op | source)
XLA Modules:
  0.0 162.1 jit_solution(743374324543547308)
XLA Ops:
  0.0 160.8 %shard_map.46 = f32[1,512,8,128]{3,2,1,0:T(8,128)S(1)} custom-call(f32[1,512,8,128]{3,2,1,0:T(8,128)} %forcing.1, f32[4,64,128]{2,1,0:T(8,128)} %initial.1, f32[4,64,128]{2,1,0:T(8,128)} %diffusion.1, f32[4,64,128]{2,1,0:T(8,128)} %drift.1), custom_call_target="tpu_custom_call" | custom-call | tf_op jit(solution)/shard_map/pallas_call | solution.py:379
  160.8 1.3 copy.6

commit v4 on v3

v4 whole, which is shorter than its diff:
```python
import jax
import jax.numpy as jnp
from jax import lax
from jax.experimental import pallas as pl
from jax.experimental.pallas import tpu as pltpu
from jax.sharding import PartitionSpec as P

NT = 16
COLS = 16
RING = 8
FIRST = 3
PIECES = 4
MESH = pl.DeviceIdType.MESH
F32 = jnp.float32


def snake(n):
    y, x = n // 4, n % 4
    return y * 4 + x + (y % 2) * (3 - 2 * x)


def remote(src, dst, send, recv, device):
    return pltpu.make_async_remote_copy(
        src_ref=src, dst_ref=dst, send_sem=send, recv_sem=recv, device_id=device, device_id_type=MESH
    )


def await_bytes(ref, sem):
    pltpu.make_async_copy(ref, ref, sem).wait()


def kernel(
    forcing, initial, diffusion, drift, out,
    G, E, D, R, DP, EP, IV, SP, W1, W2,
    csend, crecv, xsend, xrecv, fsend, frecv, gsend, grecv, hsend, hrecv, osend, orecv,
):
    t = lax.axis_index("tm")
    c = lax.axis_index("space")
    q = t // RING
    j = t % RING
    part = 2 * snake(q) + c

    def at(p, jj):
        return (snake(p // 2) * RING + jj, p % 2)

    barrier = pltpu.get_barrier_semaphore()

    def greet(device):
        pl.semaphore_signal(barrier, inc=1, device_id=device, device_id_type=MESH)

    @pl.loop(1, 2 * COLS)
    def _(n):
        greet(at((part + n) % (2 * COLS), j))

    @pl.loop(1, RING)
    def _(n):
        chip = snake(q) * RING + (j + n) % RING
        greet((chip, c))
        greet((chip, 1 - c))

    left, right = (j + RING - 1) % RING, (j + 1) % RING
    up = (part + 1) % (2 * COLS)
    down = (part + 2 * COLS - 1) % (2 * COLS)
    for jj in (left, right):
        for p in (part, up, down):
            greet(at(p, jj))

    has_left, has_right = j > 0, j < RING - 1
    has_down, has_up = part > 0, part < 2 * COLS - 1
    x_edge = jnp.logical_or(j == 0, j == RING - 1)
    z_edge = jnp.logical_or(part == 0, part == 2 * COLS - 1)
    first_rows, last_rows = pl.ds(0, 4), pl.ds(4, 4)
    own = pl.ds(4, 16)

    def clear_outside(A):
        @pl.when(part == 0)
        def _():
            A[pl.ds(0, 4)] = jnp.zeros((4, 2, 2, 8, 128), F32)

        @pl.when(part == 2 * COLS - 1)
        def _():
            A[pl.ds(20, 4)] = jnp.zeros((4, 2, 2, 8, 128), F32)

        @pl.when(j == 0)
        def _():
            A[:, 1, :, last_rows, :] = jnp.zeros((24, 2, 4, 128), F32)

        @pl.when(j == RING - 1)
        def _():
            A[:, 1, :, first_rows, :] = jnp.zeros((24, 2, 4, 128), F32)

    @pl.loop(0, NT)
    def _(k):
        clear_outside(E.at[k])
        clear_outside(G.at[k])

    pl.semaphore_wait(barrier, (2 * COLS - 1) + 2 * (RING - 1) + 6)

    def halo_copies(A, send, recv, depth):
        short = depth - 1

        def move(zs, rows, zd, tile, p, jj, group):
            remote(
                A.at[zs, 0, :, rows, :], A.at[zd, tile, :, rows, :],
                send.at[group], recv.at[group], at(p, jj),
            ).start()

        def ends(n):
            return (
                (has_up, pl.ds(20 - n, n), pl.ds(4 - n, n), up),
                (has_down, pl.ds(4, n), pl.ds(20, n), down),
            )

        for has_z, zs, zd, p in ends(short):
            @pl.when(jnp.logical_and(has_z, has_left))
            def _():
                move(zs, pl.ds(0, short), zd, 1, p, left, 2)

            @pl.when(jnp.logical_and(has_z, has_right))
            def _():
                move(zs, pl.ds(8 - short, short), zd, 1, p, right, 2)

        @pl.when(has_left)
        def _():
            move(own, pl.ds(0, depth), own, 1, part, left, 0)

        @pl.when(has_right)
        def _():
            move(own, pl.ds(8 - depth, depth), own, 1, part, right, 0)

        for has_z, zs, zd, p in ends(depth):
            @pl.when(has_z)
            def _():
                move(zs, pl.ds(0, 8), zd, 0, p, j, 1)

    def await_halos(sem, depth):
        inside = jnp.logical_not
        short = depth - 1

        def rows_of(n):
            if n % 8 == 0:
                return forcing.at[0, pl.ds(0, n // 8)]
            if n // 2 <= 24:
                return IV.at[pl.ds(0, n // 2), 0, 0, pl.ds(0, 2), :]
            return IV.at[pl.ds(0, n // 4), 0, :, pl.ds(0, 2), :]

        def await_rows(condition, group, n):
            @pl.when(condition)
            def _():
                await_bytes(rows_of(n), sem.at[group])

        await_rows(inside(x_edge), 0, 64 * depth)
        await_rows(x_edge, 0, 32 * depth)
        await_rows(inside(z_edge), 1, 32 * depth)
        await_rows(z_edge, 1, 16 * depth)
        corner = 2 * short * short
        await_rows(jnp.logical_and(inside(z_edge), inside(x_edge)), 2, 4 * corner)
        await_rows(jnp.logical_and(z_edge, inside(x_edge)), 2, 2 * corner)
        await_rows(jnp.logical_and(inside(z_edge), x_edge), 2, 2 * corner)
        await_rows(jnp.logical_and(z_edge, x_edge), 2, corner)

    def send_forcing():
        mine = G.at[q, own, 0, c]
        pltpu.make_async_copy(forcing.at[0, pl.ds(part * 16, 16)], mine, frecv.at[q]).start()

        @pl.loop(1, 2 * COLS)
        def _(n):
            p = (part + n) % (2 * COLS)
            remote(forcing.at[0, pl.ds(p * 16, 16)], mine, fsend, frecv.at[q], at(p, j)).start()

    half = j // 4
    zs = pl.ds(4 + (j % 4) * 4, 4)
    stay = jnp.logical_and(c == half, snake(q) == q)
    arriving = ((diffusion, D), (drift, R), (initial, E.at[0]))
    for a, (ref, A) in enumerate(arriving):
        for n in (4, 3, 5, 2, 6, 1, 7, 0):
            jj = (j + n) % RING
            src = ref.at[:, pl.ds(pl.multiple_of(jj * 8, 8), 8), :]
            dst = A.at[zs, 0, c]
            if n == 0:
                @pl.when(stay)
                def _():
                    pltpu.make_async_copy(src, dst, crecv.at[a]).start()

                @pl.when(jnp.logical_not(stay))
                def _():
                    remote(src, dst, csend, crecv.at[a], (snake(q) * RING + j, half)).start()
            else:
                remote(src, dst, csend, crecv.at[a], (snake(q) * RING + jj, half)).start()

    @pl.when(q < FIRST)
    def _():
        send_forcing()

    for a, (ref, A) in enumerate(arriving):
        await_bytes(forcing.at[0, pl.ds(0, 32)], crecv.at[a])
        if a < 2:
            halo_copies(A, xsend.at[a], xrecv.at[a], 3)
        else:
            halo_copies(A, hsend.at[0], hrecv.at[0], 4)

    await_halos(xrecv.at[0], 3)
    await_halos(xrecv.at[1], 3)
    for z in range(0, 24, 4):
        s = pl.ds(z, 4)
        d, r = D[s], R[s]
        inv = 1.0 / (1.0 + 6.0 * d + r)
        IV[s] = inv
        DP[s] = d * inv
        EP[s] = (d + r) * inv
    for A in (IV, DP, EP):
        clear_outside(A)

    def send_force(k):
        halo_copies(G.at[k], gsend.at[k], grecv.at[k], 3)

    def await_force(k):
        await_bytes(forcing.at[0, pl.ds(0, 32)], frecv.at[k])

    await_force(0)
    send_force(0)

    @pl.when(q >= FIRST)
    def _():
        send_forcing()

    def relax(load, load_s, z, n, tiles):
        shape = (n, 8, 128)
        row = lax.broadcasted_iota(jnp.int32, shape, 1)
        lane = lax.broadcasted_iota(jnp.int32, shape, 2)
        first_row, last_row = row == 0, row == 7
        first_lane, last_lane = lane == 0, lane == 127
        zero = jnp.zeros(shape, F32)
        wide = [[load(z - 1, n + 2, T, h) for h in range(2)] for T in range(tiles)]
        mid = [[wide[T][h][1:-1] for h in range(2)] for T in range(tiles)]
        if tiles == 1:
            mid.append([load(z, n, 1, h) for h in range(2)])
        result = [[None, None] for T in range(tiles)]
        beside = [[None, None] for T in range(tiles)]
        for h in range(2):
            a = [pltpu.roll(mid[T][h], 1, 1) for T in range(2)]
            b = [pltpu.roll(mid[T][h], 7, 1) for T in range(2)]
            for T in range(tiles):
                beside[T][h] = jnp.where(first_row, a[1 - T], a[T]) + jnp.where(last_row, b[1 - T], b[T])
        for T in range(tiles):
            a0, a1 = pltpu.roll(mid[T][0], 1, 2), pltpu.roll(mid[T][1], 1, 2)
            b0, b1 = pltpu.roll(mid[T][0], 127, 2), pltpu.roll(mid[T][1], 127, 2)
            across = (
                jnp.where(first_lane, zero, a0) + jnp.where(last_lane, b1, b0),
                jnp.where(first_lane, a0, a1) + jnp.where(last_lane, zero, b1),
            )
            for h in range(2):
                total = beside[T][h] + across[h] + wide[T][h][2:]
                s = pl.ds(z, n)
                result[T][h] = (
                    load_s(z, n, T, h) + DP[s, T, h] * total + EP[s, T, h] * wide[T][h][:-2]
                )
        return result

    def chunks(first, last):
        z = first
        while z < last:
            n = min(4, last - z)
            yield z, n
            z += n

    def from_ref(A):
        return lambda z, n, T, h: A[pl.ds(z, n), T, h]

    def send_state(k, piece):
        rows = 16 // PIECES
        for h in range(2):
            src = E.at[k + 1, pl.ds(4 + piece * rows, rows), 0, h]
            dst = out.at[0, pl.ds(part * 16 + piece * rows, rows)]
            mine = jnp.logical_and(k == q, c == h)

            @pl.when(mine)
            def _():
                pltpu.make_async_copy(src, dst, orecv).start()

            @pl.when(jnp.logical_not(mine))
            def _():
                remote(src, dst, osend, orecv, (k * RING + j, h)).start()

    @pl.loop(0, NT)
    def _(k):
        now, later = E.at[k], E.at[k + 1]
        force = G.at[k]
        await_halos(grecv.at[k], 3)
        await_halos(hrecv.at[k], 4)

        def make_source(z, n, T, h):
            s = pl.ds(z, n)
            v = (now[s, T, h] + force[s, T, h]) * IV[s, T, h]
            SP[s, T, h] = v
            return v

        for load, load_s, W, margin in (
            (from_ref(now), make_source, W1, 1),
            (from_ref(W1), from_ref(SP), W2, 2),
            (from_ref(W2), from_ref(SP), W1, 3),
        ):
            for z, n in chunks(margin, 24 - margin):
                v = relax(load, load_s, z, n, 2)
                for T in range(2):
                    for h in range(2):
                        W[pl.ds(z, n), T, h] = v[T][h]

        for z, n in chunks(4, 20):
            v = relax(from_ref(W1), from_ref(SP), z, n, 1)
            for h in range(2):
                later[pl.ds(z, n), 0, h] = v[0][h]

        @pl.when(k < NT - 1)
        def _():
            halo_copies(later, hsend.at[k + 1], hrecv.at[k + 1], 4)

        for d in range(PIECES):
            @pl.when(k >= d)
            def _():
                send_state(k - d, d)

        @pl.when(k == 0)
        def _():
            await_halos(hsend.at[0], 4)
            await_force(1)

        @pl.when(k < NT - 2)
        def _():
            await_force(k + 2)

        @pl.when(k < NT - 1)
        def _():
            await_halos(hsend.at[k + 1], 4)

        @pl.when(k == 0)
        def _():
            send_force(1)

        @pl.when(k < NT - 2)
        def _():
            send_force(k + 2)

    for k in range(NT - PIECES + 1, NT):
        for piece in range(NT - k, PIECES):
            send_state(k, piece)

    @pl.when(stay)
    def _():
        await_bytes(forcing.at[0, pl.ds(0, 84)], csend)

    @pl.when(jnp.logical_not(stay))
    def _():
        await_bytes(forcing.at[0, pl.ds(0, 96)], csend)

    await_halos(xsend.at[0], 3)
    await_halos(xsend.at[1], 3)

    @pl.loop(0, NT)
    def _(k):
        await_halos(gsend.at[k], 3)

    await_bytes(forcing.at[0, pl.ds(0, 496)], fsend)
    await_bytes(forcing.at[0, pl.ds(0, 496)], osend)
    await_bytes(out, orecv)


def per_device(forcing, initial, diffusion, drift):
    wide = (24, 2, 2, 8, 128)
    vmem = lambda *shape: pltpu.VMEM(shape, F32)
    dma = pltpu.SemaphoreType.DMA
    return pl.pallas_call(
        kernel,
        out_shape=jax.ShapeDtypeStruct(forcing.shape, F32),
        in_specs=[pl.BlockSpec(memory_space=pltpu.HBM)] * 4,
        out_specs=pl.BlockSpec(memory_space=pl.ANY),
        scratch_shapes=[vmem(NT, *wide), vmem(NT + 1, *wide)]
        + [vmem(*wide)] * 8
        + [dma, dma((3,)), dma((2, 3)), dma((2, 3)), dma, dma((NT,)), dma((NT, 3)), dma((NT, 3))]
        + [dma((NT, 3)), dma((NT, 3)), dma, dma],
        compiler_params=pltpu.CompilerParams(
            collective_id=0, has_side_effects=True, vmem_limit_bytes=40 * 1024 * 1024
        ),
    )(*[pltpu.with_memory_space_constraint(a, pltpu.HBM) for a in (forcing, initial, diffusion, drift)])


def solution(mesh):
    in_specs = (
        P("tm", None, None, "space"),
        P("tm", None, "space"),
        P("tm", None, "space"),
        P("tm", None, "space"),
    )
    out_specs = P("tm", None, None, "space")
    return jax.shard_map(
        per_device, mesh=mesh, in_specs=in_specs, out_specs=out_specs, check_vma=False
    )
```

time: 162 us -> 156 us (0.963)
  Pallas kernels: 161 us -> 155 us
    pallas_call x1, Pallas kernels: 161 us -> 155 us  [per_device(): pl.pallas_call(kernel, out_shape=jax.ShapeDtypeStruct(forcing.shape, F32)...]
where the time goes in v4:
time: 156 us
  Pallas kernels  155 us (99%)
    pallas_call x1, Pallas kernels, per_device(): pl.pallas_call(kernel, out_shape=jax.ShapeDtypeStruct(forcing.shape, F32)...  155 us

profile of v4, /device:TPU:31, one launch (start us, length us, event | category | flops | bytes accessed | tf_op | source)
XLA Modules:
  0.0 155.8 jit_solution(16814167531007030923)
XLA Ops:
  0.0 154.5 %shard_map.46 = f32[1,512,8,128]{3,2,1,0:T(8,128)S(1)} custom-call(f32[1,512,8,128]{3,2,1,0:T(8,128)} %forcing.1, f32[4,64,128]{2,1,0:T(8,128)} %initial.1, f32[4,64,128]{2,1,0:T(8,128)} %diffusion.1, f32[4,64,128]{2,1,0:T(8,128)} %drift.1), custom_call_target="tpu_custom_call" | custom-call | tf_op jit(solution)/shard_map/pallas_call | solution.py:372
  154.5 1.3 copy.6

commit v5 on v4

--- a/solution.py
+++ b/solution.py
@@ -8,7 +8,6 @@
 NT = 16
 COLS = 16
 RING = 8
-FIRST = 3
 PIECES = 4
 MESH = pl.DeviceIdType.MESH
 F32 = jnp.float32
@@ -165,7 +164,7 @@
 
         @pl.loop(1, 2 * COLS)
         def _(n):
-            p = (part + n) % (2 * COLS)
+            p = (part + 13 * n) % (2 * COLS)
             remote(forcing.at[0, pl.ds(p * 16, 16)], mine, fsend, frecv.at[q], at(p, j)).start()
 
     half = j // 4
@@ -188,9 +187,7 @@
             else:
                 remote(src, dst, csend, crecv.at[a], (snake(q) * RING + jj, half)).start()
 
-    @pl.when(q < FIRST)
-    def _():
-        send_forcing()
+    send_forcing()
 
     for a, (ref, A) in enumerate(arriving):
         await_bytes(forcing.at[0, pl.ds(0, 32)], crecv.at[a])
@@ -219,10 +216,6 @@
 
     await_force(0)
     send_force(0)
-
-    @pl.when(q >= FIRST)
-    def _():
-        send_forcing()
 
     def relax(load, load_s, z, n, tiles):
         shape = (n, 8, 128)

time: 156 us -> 146 us (0.936)
  Pallas kernels: 155 us -> 145 us
    pallas_call x1, Pallas kernels: 155 us -> 145 us  [per_device(): pl.pallas_call(kernel, out_shape=jax.ShapeDtypeStruct(forcing.shape, F32)...]
where the time goes in v5:
time: 146 us
  Pallas kernels  145 us (99%)
    pallas_call x1, Pallas kernels, per_device(): pl.pallas_call(kernel, out_shape=jax.ShapeDtypeStruct(forcing.shape, F32)...  145 us

profile of v5, /device:TPU:31, one launch (start us, length us, event | category | flops | bytes accessed | tf_op | source)
XLA Modules:
  0.0 146.1 jit_solution(4833036888948189402)
XLA Ops:
  0.0 144.8 %shard_map.46 = f32[1,512,8,128]{3,2,1,0:T(8,128)S(1)} custom-call(f32[1,512,8,128]{3,2,1,0:T(8,128)} %forcing.1, f32[4,64,128]{2,1,0:T(8,128)} %initial.1, f32[4,64,128]{2,1,0:T(8,128)} %diffusion.1, f32[4,64,128]{2,1,0:T(8,128)} %drift.1), custom_call_target="tpu_custom_call" | custom-call | tf_op jit(solution)/shard_map/pallas_call | solution.py:365
  144.8 1.3 copy.6

commit v6 on v5

--- a/solution.py
+++ b/solution.py
@@ -95,7 +95,7 @@
 
     pl.semaphore_wait(barrier, (2 * COLS - 1) + 2 * (RING - 1) + 6)
 
-    def halo_copies(A, send, recv, depth):
+    def halo_copies(A, send, recv, depth, stage=None):
         short = depth - 1
 
         def move(zs, rows, zd, tile, p, jj, group):
@@ -110,7 +110,7 @@
                 (has_down, pl.ds(4, n), pl.ds(20, n), down),
             )
 
-        for has_z, zs, zd, p in ends(short):
+        for has_z, zs, zd, p in () if stage == 1 else ends(short):
             @pl.when(jnp.logical_and(has_z, has_left))
             def _():
                 move(zs, pl.ds(0, short), zd, 1, p, left, 2)
@@ -118,6 +118,9 @@
             @pl.when(jnp.logical_and(has_z, has_right))
             def _():
                 move(zs, pl.ds(8 - short, short), zd, 1, p, right, 2)
+
+        if stage == 0:
+            return
 
         @pl.when(has_left)
         def _():
@@ -158,11 +161,12 @@
         await_rows(jnp.logical_and(inside(z_edge), x_edge), 2, 2 * corner)
         await_rows(jnp.logical_and(z_edge, x_edge), 2, corner)
 
-    def send_forcing():
+    def send_forcing(first, last):
         mine = G.at[q, own, 0, c]
-        pltpu.make_async_copy(forcing.at[0, pl.ds(part * 16, 16)], mine, frecv.at[q]).start()
-
-        @pl.loop(1, 2 * COLS)
+        if first == 1:
+            pltpu.make_async_copy(forcing.at[0, pl.ds(part * 16, 16)], mine, frecv.at[q]).start()
+
+        @pl.loop(first, last)
         def _(n):
             p = (part + 13 * n) % (2 * COLS)
             remote(forcing.at[0, pl.ds(p * 16, 16)], mine, fsend, frecv.at[q], at(p, j)).start()
@@ -187,7 +191,11 @@
             else:
                 remote(src, dst, csend, crecv.at[a], (snake(q) * RING + jj, half)).start()
 
-    send_forcing()
+    send_forcing(1, 16)
+
+    @pl.when(q < 4)
+    def _():
+        send_forcing(16, 2 * COLS)
 
     for a, (ref, A) in enumerate(arriving):
         await_bytes(forcing.at[0, pl.ds(0, 32)], crecv.at[a])
@@ -195,6 +203,10 @@
             halo_copies(A, xsend.at[a], xrecv.at[a], 3)
         else:
             halo_copies(A, hsend.at[0], hrecv.at[0], 4)
+
+    @pl.when(q >= 4)
+    def _():
+        send_forcing(16, 2 * COLS)
 
     await_halos(xrecv.at[0], 3)
     await_halos(xrecv.at[1], 3)
@@ -299,14 +311,19 @@
                     for h in range(2):
                         W[pl.ds(z, n), T, h] = v[T][h]
 
-        for z, n in chunks(4, 20):
+        for z, n in ((4, 4), (16, 4), (8, 4), (12, 4)):
+            if z == 8:
+                @pl.when(k < NT - 1)
+                def _():
+                    halo_copies(later, hsend.at[k + 1], hrecv.at[k + 1], 4, 0)
+
             v = relax(from_ref(W1), from_ref(SP), z, n, 1)
             for h in range(2):
                 later[pl.ds(z, n), 0, h] = v[0][h]
 
         @pl.when(k < NT - 1)
         def _():
-            halo_copies(later, hsend.at[k + 1], hrecv.at[k + 1], 4)
+            halo_copies(later, hsend.at[k + 1], hrecv.at[k + 1], 4, 1)
 
         for d in range(PIECES):
             @pl.when(k >= d)

time: 146 us -> 144 us (0.986)
  Pallas kernels: 145 us -> 143 us
    pallas_call x1, Pallas kernels: 145 us -> 143 us  [per_device(): pl.pallas_call(kernel, out_shape=jax.ShapeDtypeStruct(forcing.shape, F32)...]
where the time goes in v6:
time: 144 us
  Pallas kernels  143 us (99%)
    pallas_call x1, Pallas kernels, per_device(): pl.pallas_call(kernel, out_shape=jax.ShapeDtypeStruct(forcing.shape, F32)...  143 us

profile of v6, /device:TPU:31, one launch (start us, length us, event | category | flops | bytes accessed | tf_op | source)
XLA Modules:
  0.0 144.1 jit_solution(1073260091678520640)
XLA Ops:
  0.0 142.8 %shard_map.46 = f32[1,512,8,128]{3,2,1,0:T(8,128)S(1)} custom-call(f32[1,512,8,128]{3,2,1,0:T(8,128)} %forcing.1, f32[4,64,128]{2,1,0:T(8,128)} %initial.1, f32[4,64,128]{2,1,0:T(8,128)} %diffusion.1, f32[4,64,128]{2,1,0:T(8,128)} %drift.1), custom_call_target="tpu_custom_call" | custom-call | tf_op jit(solution)/shard_map/pallas_call | solution.py:382
  142.8 1.3 copy.6

commit v7 on v6

--- a/solution.py
+++ b/solution.py
@@ -119,6 +119,11 @@
             def _():
                 move(zs, pl.ds(8 - short, short), zd, 1, p, right, 2)
 
+        for has_z, zs, zd, p in () if stage == 1 else ends(depth):
+            @pl.when(has_z)
+            def _():
+                move(zs, pl.ds(0, 8), zd, 0, p, j, 1)
+
         if stage == 0:
             return
 
@@ -129,11 +134,6 @@
         @pl.when(has_right)
         def _():
             move(own, pl.ds(8 - depth, depth), own, 1, part, right, 0)
-
-        for has_z, zs, zd, p in ends(depth):
-            @pl.when(has_z)
-            def _():
-                move(zs, pl.ds(0, 8), zd, 0, p, j, 1)
 
     def await_halos(sem, depth):
         inside = jnp.logical_not

time: 144 us -> 144 us (level)
  no operation moved by 1% of the time
where the time goes in v7:
time: 144 us
  Pallas kernels  143 us (99%)
    pallas_call x1, Pallas kernels, per_device(): pl.pallas_call(kernel, out_shape=jax.ShapeDtypeStruct(forcing.shape, F32)...  143 us

profile of v7, /device:TPU:31, one launch (start us, length us, event | category | flops | bytes accessed | tf_op | source)
XLA Modules:
  0.0 144.1 jit_solution(10521876432048978603)
XLA Ops:
  0.0 142.7 %shard_map.46 = f32[1,512,8,128]{3,2,1,0:T(8,128)S(1)} custom-call(f32[1,512,8,128]{3,2,1,0:T(8,128)} %forcing.1, f32[4,64,128]{2,1,0:T(8,128)} %initial.1, f32[4,64,128]{2,1,0:T(8,128)} %diffusion.1, f32[4,64,128]{2,1,0:T(8,128)} %drift.1), custom_call_target="tpu_custom_call" | custom-call | tf_op jit(solution)/shard_map/pallas_call | solution.py:382
  142.8 1.3 copy.6
